TPU v7x, 128 devices: a whole 4x4x4 slice. The times are simulated.
128 devices in a mesh: head: 16 (over y, z), seq: 8 (over x, core).
Axes of the slice: x: 4, y: 4, z: 4, core: 2. Of those that a mesh axis runs over, the one named last changes fastest.
Arguments:
- query_rows: bfloat16 [2, 8192, 4096], P(None, ('seq', 'head')), may hold values from -6 to 6
- key_rows: bfloat16 [2, 8192, 4096], P(None, ('seq', 'head')), may hold values from -6 to 6
- value_rows: bfloat16 [2, 8192, 4096], P(None, ('seq', 'head')), may hold values from -6 to 6
- beta_raw: bfloat16 [2, 8192, 32], P(None, ('seq', 'head')), may hold values from -5 to 5
- gate_latent: bfloat16 [2, 8192, 128], P(None, ('seq', 'head')), may hold values from -3 to 3
- gate_up: bfloat16 [128, 4096], replicated, may hold values from -1 to 1
- dt_bias: float32 [2, 4096], replicated, may hold values from -13 to -1
- decay_log: float32 [32], replicated, may hold values from -0.5 to 0.5
- boundary: int32 [2, 8192], P(None, ('seq', 'head')), may hold values 0 or 1
- modality: int32 [2, 8192], P(None, ('seq', 'head')), may hold values from 0 to 1, as said below
- out_gate: bfloat16 [2, 8192, 4096], P(None, ('seq', 'head')), may hold values from -6 to 6
- norm_gain: float32 [4096], replicated, may hold values from 0.1 to 1.9
Outputs:
- mixed_out: bfloat16 [2, 8192, 4096], P(None, ('seq', 'head'))
Inputs may be any that keep to these rules, and one draw needn't show every extreme that they name: `modality`: each sequence has runs of audio and runs of text; the value changes at a few positions.
All inputs are finite; a program needn't handle non-finite values. No bound on the sum of `boundary` on one device may be relied on, other than what follows from the above.
Results may differ from a plain program's by a relative error of at most 0.0049.
Values may be sent and summed in bfloat16 or wider, within the bound.
A program may use at most 128 MiB of HBM per device.

v0:
```python
import jax
import jax.numpy as jnp
from jax import lax
from jax.sharding import PartitionSpec as P

H = 32
DK = 128
RANK = 128
BLOCK = 128


exact_mode = lax.Precision.HIGHEST
norm_eps = 1e-06


def in_one_piece(arrays, axis, split_dim, concat_dim, along):
    widths = [a.shape[along] for a in arrays]
    both = jnp.concatenate(arrays, axis=along)
    out = lax.all_to_all(both, axis, split_axis=split_dim, concat_axis=concat_dim, tiled=True)
    return tuple(jnp.split(out, [sum(widths[:k]) for k in range(1, len(widths))], axis=along))


def joined_along(parts, dim):
    lengths = list(parts.shape[1:])
    lengths[dim] *= parts.shape[0]
    return jnp.moveaxis(parts, 0, dim).reshape(lengths)


def copy_for_each(array, axis):
    copies = jnp.broadcast_to(array, (lax.axis_size(axis), *array.shape))
    return lax.all_to_all(copies, axis, split_axis=0, concat_axis=0, tiled=True)


def gathered_copies(array, axis, dim):
    return joined_along(copy_for_each(array, axis), dim)


def side_by_side(arrays, axis, dim, along):
    widths = [a.shape[along] for a in arrays]
    both = jnp.concatenate(arrays, axis=along)
    out = gathered_copies(both, axis, dim)
    return tuple(jnp.split(out, [sum(widths[:k]) for k in range(1, len(widths))], axis=along))


def prefix(part, axis, combine, identity):
    place = lax.axis_index(axis)
    gathered = jax.tree.map(lambda a: lax.all_gather(a, axis), part)
    state = jax.tree.map(lambda a, e: jnp.zeros_like(a) + jnp.asarray(e, a.dtype), part, identity)

    def one(hop, state):
        return combine(
            state, jax.tree.map(lambda a: lax.dynamic_index_in_dim(a, hop, 0, False), gathered)
        )

    return lax.fori_loop(0, place, one, state)


def product(left_side, right_side):
    return jnp.matmul(left_side, right_side, precision=exact_mode)


def unit_rows(matrix):
    return matrix * lax.rsqrt(jnp.sum(matrix * matrix, axis=-1, keepdims=True) + norm_eps)


def invert_unit_lower(strict):
    length = strict.shape[-1]
    unit_mat = jnp.eye(length, dtype=jnp.float32)
    nil_power = -strict
    result = unit_mat + nil_power
    for repeat in range(1, length.bit_length() - 1):
        nil_power = product(nil_power, nil_power)
        result = product(result, unit_mat + nil_power)
    return result


def block_parts(query_block, key_block, value_block, beta_block, decay_block, mark_block):
    length = query_block.shape[-2]
    decay_sum = jnp.cumsum(decay_block, axis=-2)
    counts = jnp.cumsum(mark_block, axis=-1)
    alive_rows = (counts == 0).astype(jnp.float32)
    same_doc = (counts[..., :, None] == counts[..., None, :]).astype(jnp.float32)
    row_ids = lax.broadcasted_iota(jnp.int32, (length, length), 0)
    col_ids = lax.broadcasted_iota(jnp.int32, (length, length), 1)
    strict_low = (row_ids > col_ids).astype(jnp.float32)
    with_diag = (row_ids >= col_ids).astype(jnp.float32)
    growth = jnp.exp(decay_sum)
    key_grow = key_block * growth
    key_shrink = key_block * jnp.exp(-decay_sum)
    key_gram = jnp.einsum("...ik,...jk->...ij", key_grow, key_shrink, precision=exact_mode)
    strict = key_gram * strict_low * same_doc * beta_block[..., :, None]
    solver = invert_unit_lower(strict) * beta_block[..., None, :]
    weight_rows = product(solver, key_grow * alive_rows[..., :, None])
    pseudo_rows = product(solver, value_block)
    query_grow = query_block * growth
    mixing = (
        jnp.einsum("...ik,...jk->...ij", query_grow, key_shrink, precision=exact_mode)
        * with_diag
        * same_doc
    )
    query_live = query_grow * alive_rows[..., :, None]
    last_sum = decay_sum[..., -1:, :]
    key_tail = key_block * jnp.exp(last_sum - decay_sum) * same_doc[..., -1, :][..., :, None]
    carry_decay = jnp.exp(last_sum[..., 0, :]) * alive_rows[..., -1:]
    return (weight_rows, pseudo_rows, mixing, query_live, key_tail, carry_decay)


def compose(earlier, latter):
    return (product(latter[0], earlier[0]), product(latter[0], earlier[1]) + latter[1])


def per_device(
    query_rows,
    key_rows,
    value_rows,
    beta_raw,
    gate_latent,
    gate_up,
    dt_bias,
    decay_log,
    boundary,
    modality,
    out_gate,
    norm_gain,
):
    groups = lax.axis_size("head")
    seq_count, tok_rows, columns = query_rows.shape
    heads_here = H // groups
    group_width = heads_here * DK
    group_start = lax.axis_index("head")
    query_here, key_here, value_here, beta_here = (
        *in_one_piece((query_rows, key_rows, value_rows), "head", 2, 1, 0),
        lax.all_to_all(beta_raw, "head", split_axis=2, concat_axis=1, tiled=True),
    )
    latent_here, mark_here, kind_here = (
        gathered_copies(gate_latent, "head", 1),
        *side_by_side((boundary, modality), "head", 1, 0),
    )
    gate_cols = lax.dynamic_slice_in_dim(gate_up, group_start * group_width, group_width, 1)
    gate_here = jnp.dot(
        latent_here.reshape(-1, RANK), gate_cols, preferred_element_type=jnp.float32
    )
    gate_here = gate_here.astype(jnp.bfloat16).reshape(seq_count, latent_here.shape[1], group_width)
    span_rows = query_here.shape[1]
    blocks = span_rows // BLOCK
    bias_cols = lax.dynamic_slice_in_dim(dt_bias, group_start * group_width, group_width, 1)
    gate_bias = jnp.where(kind_here[..., None] == 1, bias_cols[1], bias_cols[0])
    rate_scale = jnp.repeat(
        jnp.exp(lax.dynamic_slice_in_dim(decay_log, group_start * heads_here, heads_here, 0)), DK
    )
    log_decay = -rate_scale * jax.nn.softplus(gate_here.astype(jnp.float32) + gate_bias)

    def to_blocks(tensor):
        return tensor.reshape(seq_count, blocks, BLOCK, heads_here, DK).transpose(0, 3, 1, 2, 4)

    unit_query = to_blocks(
        unit_rows(query_here.astype(jnp.float32).reshape(seq_count, span_rows, heads_here, DK))
        * DK ** (-0.5)
    )
    unit_key = to_blocks(
        unit_rows(key_here.astype(jnp.float32).reshape(seq_count, span_rows, heads_here, DK))
    )
    value_blocks = to_blocks(value_here.astype(jnp.float32))
    decay_blocks = to_blocks(log_decay)
    beta_blocks = (
        jax.nn.sigmoid(beta_here.astype(jnp.float32))
        .reshape(seq_count, blocks, BLOCK, heads_here)
        .transpose(0, 3, 1, 2)
    )
    mark_blocks = jnp.broadcast_to(
        mark_here.reshape(seq_count, 1, blocks, BLOCK), (seq_count, heads_here, blocks, BLOCK)
    )
    weight_rows, pseudo_rows, mixing, query_live, key_tail, carry_decay = block_parts(
        unit_query, unit_key, value_blocks, beta_blocks, decay_blocks, mark_blocks
    )
    unit_mat = jnp.eye(DK, dtype=jnp.float32)
    move_mats = carry_decay[..., :, None] * unit_mat - jnp.einsum(
        "...ck,...cl->...kl", key_tail, weight_rows, precision=exact_mode
    )
    offsets = jnp.einsum("...ck,...cv->...kv", key_tail, pseudo_rows, precision=exact_mode)
    inclusive = lax.associative_scan(compose, (move_mats, offsets), axis=2)
    span_move = inclusive[0][:, :, -1]
    span_offset = inclusive[1][:, :, -1]
    identity = (jnp.broadcast_to(unit_mat, span_move.shape), jnp.zeros_like(span_offset))
    before_move, incoming = prefix((span_move, span_offset), "seq", compose, identity)
    first_move = jnp.broadcast_to(unit_mat, (seq_count, heads_here, 1, DK, DK))
    prior_move = jnp.concatenate([first_move, inclusive[0][:, :, :-1]], axis=2)
    prior_offset = jnp.concatenate([jnp.zeros_like(first_move), inclusive[1][:, :, :-1]], axis=2)
    states = product(prior_move, incoming[:, :, None]) + prior_offset
    fresh_rows = pseudo_rows - product(weight_rows, states)
    core_out = product(query_live, states) + product(mixing, fresh_rows)
    core_rows = (
        core_out.transpose(0, 2, 3, 1, 4)
        .reshape(seq_count, span_rows, group_width)
        .astype(jnp.bfloat16)
    )
    returned = lax.all_to_all(core_rows, "head", split_axis=1, concat_axis=2, tiled=True)
    core_wide = returned.astype(jnp.float32).reshape(seq_count, tok_rows, H, DK)
    normed = core_wide * lax.rsqrt(
        jnp.mean(core_wide * core_wide, axis=-1, keepdims=True) + norm_eps
    )
    mixed_out = (
        normed.reshape(seq_count, tok_rows, columns)
        * norm_gain
        * jax.nn.sigmoid(out_gate.astype(jnp.float32))
    )
    return mixed_out.astype(jnp.bfloat16)


def solution(mesh):
    return jax.shard_map(
        per_device,
        mesh=mesh,
        in_specs=(
            P(None, ("seq", "head"), None),
            P(None, ("seq", "head"), None),
            P(None, ("seq", "head"), None),
            P(None, ("seq", "head"), None),
            P(None, ("seq", "head"), None),
            P(),
            P(),
            P(),
            P(None, ("seq", "head")),
            P(None, ("seq", "head")),
            P(None, ("seq", "head"), None),
            P(),
        ),
        out_specs=P(None, ("seq", "head"), None),
        check_vma=False,
    )
```

profile of v0, /device:TPU:6, one launch (start us, length us, event | category | flops | bytes accessed | tf_op | source)
XLA Modules:
  0.0 398.6 jit_solution(11563325329879583719)
XLA Ops:
  8.1 8.0 %all-to-all-start.3 = ((bf16[16,2,128]{2,1,0:T(2,128)(2,1)}), bf16[16,2,128]{2,1,0:T(2,128)(2,1)S(1)}, u32[]{:S(2)}, u32[]{:S(2)}) async-start(bf16[16,2,128]{2,1,0:T(2,128)(2,1)} %reshape.176), calls=%async_computation.3 | async-start | bytes 16384 | tf_op jit(solution)/shard_map/all_to_all | solution.py:133
  17.0 6.7 %all-to-all-done.3 = bf16[16,2,128]{2,1,0:T(2,128)(2,1)S(1)} async-done(((bf16[16,2,128]{2,1,0:T(2,128)(2,1)}), bf16[16,2,128]{2,1,0:T(2,128)(2,1)S(1)}, u32[]{:S(2)}, u32[]{:S(2)}) %all-to-all-start.3) | async-done | bytes 8224 | tf_op jit(solution)/shard_map/all_to_all | solution.py:133
  23.7 10.6 %all_to_all.43 = s32[16,1,256]{2,1,0:T(1,128)S(1)} all-to-all(s32[16,1,256]{2,1,0:T(1,128)S(1)} %reshape.172), channel_id=1, replica_groups=mesh['head'=16,'seq'=8] {'head'}, dimensions={0} | all-to-all | bytes 32768 | tf_op jit(solution)/shard_map/all_to_all | solution.py:31
  35.9 3.6 all-to-all-start.1
  42.6 9.8 %copy.163 = bf16[6,64,4096]{1,0,2:T(8,128)(2,1)} copy(bf16[6,64,4096]{2,1,0:T(8,128)(2,1)} %pad_maximum_fusion) | data formatting | bytes 6291456 | tf_op jit(solution)/shard_map/concatenate | solution.py:18
  52.4 13.5 %reshape.174 = bf16[16,2,49152]{2,1,0:T(2,128)(2,1)} reshape(bf16[4096,6,64]{2,1,0:T(8,128)(2,1)} %bitcast.159) | data formatting | bytes 6291456
  65.9 7.3 %all-to-all-start = ((bf16[16,2,49152]{2,1,0:T(2,128)(2,1)}), bf16[16,2,49152]{2,1,0:T(2,128)(2,1)}, u32[]{:S(2)}, u32[]{:S(2)}) async-start(bf16[16,2,49152]{2,1,0:T(2,128)(2,1)} %reshape.174), calls=%async_computation | async-start | bytes 6291456 | tf_op jit(solution)/shard_map/all_to_all | solution.py:19
  87.4 23.9 %all-to-all-done = bf16[16,2,49152]{2,1,0:T(2,128)(2,1)} async-done(((bf16[16,2,49152]{2,1,0:T(2,128)(2,1)}), bf16[16,2,49152]{2,1,0:T(2,128)(2,1)}, u32[]{:S(2)}, u32[]{:S(2)}) %all-to-all-start) | async-done | bytes 3145760 | tf_op jit(solution)/shard_map/all_to_all | solution.py:19
  111.3 13.0 %reshape.175 = bf16[4096,6,64]{2,1,0:T(8,128)(2,1)} reshape(bf16[16,2,49152]{2,1,0:T(2,128)(2,1)} %all-to-all-done) | data formatting | bytes 6291456
  124.4 9.1 %copy.164 = bf16[6,64,16,256]{3,1,2,0:T(8,128)(2,1)} copy(bf16[6,64,16,256]{1,0,3,2:T(8,128)(2,1)} %bitcast.160) | data formatting | bytes 6291456 | tf_op jit(solution)/shard_map/all_to_all | solution.py:19
  133.5 4.3 %fusion.106 = (f32[2,16,64,256]{3,2,1,0:T(8,128)}, f32[2,16,64,256]{3,2,1,0:T(8,128)}) fusion(bf16[6,16,64,256]{3,2,1,0:T(8,128)(2,1)} %bitcast.161), kind=kLoop, calls=%fused_computation.136 | loop fusion | flops 2097152 | bytes 6291456 | tf_op jit(solution)/shard_map/mul | solution.py:63
  143.7 4.9 %reduce_sum.27 = f32[2,1024,2]{2,1,0:T(8,128)} reduce(f32[2,1024,2,128]{3,2,1,0:T(2,128)} %mul.206, f32[]{:T(128)} %constant.23.clone.1), dimensions={3}, to_apply=%region_0.1 | reduce | flops 520192 | bytes 2113540 | tf_op jit(solution)/shard_map/reduce_sum | solution.py:63
  155.0 4.9 %reduce_sum.28 = f32[2,1024,2]{2,1,0:T(8,128)} reduce(f32[2,1024,2,128]{3,2,1,0:T(2,128)} %mul.225, f32[]{:T(128)} %constant.23.clone.1), dimensions={3}, to_apply=%region_3.4 | reduce | flops 520192 | bytes 2113540 | tf_op jit(solution)/shard_map/reduce_sum | solution.py:63
  171.5 8.1 %broadcast_multiply_fusion = (f32[2,2,8,128,128]{4,2,3,1,0:T(8,128)S(1)}, f32[2,2,8,128,128]{4,2,3,1,0:T(8,128)S(1)}, f32[2,2,8,128,128]{4,2,3,1,0:T(8,128)}, f3...) fusion(f32[2,2,8,128]{2,3,1,0:T(8,128)} %copy.172, ...), kind=kLoop, calls=%fused_computation.104 | loop fusion | flops 6291456 | bytes 18956288 | tf_op jit(solution)/shard_map/mul | solution.py:93
  179.6 4.8 %multiply_negate_fusion = f32[2,2,8,128,128]{4,3,2,1,0:T(8,128)S(1)} fusion(f32[2,2,8,128,128]{4,2,3,1,0:T(8,128)S(1)} %get-tuple-element.65, f32[2,2,8,128,128]{4,2,3,1,0:T(8,128)S(1)} %get-tuple-element.63, f32[2,2,8,128]{3,2,1,0:T(8,128)S(1)} %bitcast.172, f32[128,128]{1,0:T(8,128)S(1)} %fusion.119, s32[2,2,8,128]{3,2,1,0:T(8,128)S(1)} %reduce_window_sum.23), kind=kOutput, calls=%fused_computation.51 | convolution fusion | flops 807927808 | bytes 6389760 | tf_op jit(solution)/shard_map/...ik,...jk->...ij/dot_general | solution.py:90
  211.6 3.7 fusion.17
  220.2 4.6 %fusion.136 = f32[2,2,8,128,128]{4,3,2,1,0:T(8,128)S(1)} fusion(f32[2,2,8,128,128]{3,4,2,1,0:T(8,128)S(1)} %copy.182, f32[2,2,8,128,128]{4,3,2,1,0:T(8,128)} %fusion.49), kind=kOutput, calls=%fused_computation.184 | convolution fusion | flops 805306368 | bytes 6291456 | tf_op jit(solution)/shard_map/...ck,...cv->...kv/dot_general | solution.py:180
  224.8 4.7 %multiply_subtract_fusion = f32[2,2,8,128,128]{4,3,2,1,0:T(8,128)S(1)} fusion(f32[2,2,8,128,128]{3,4,2,1,0:T(8,128)} %copy-done.5, f32[2,2,8,128,128]{4,3,2,1,0:T(8,128)S(1)} %copy-done.3, f32[128,128]{1,0:T(8,128)S(1)} %fusion.118, f32[2,2,8,128]{3,2,1,0:T(8,128)S(1)} %copy-done.21), kind=kOutput, calls=%fused_computation.52 | convolution fusion | flops 806354944 | bytes 6373376 | tf_op jit(solution)/shard_map/...ck,...cl->...kl/dot_general | solution.py:177
  235.9 5.8 %pad.47 = f32[2,2,4,128,128]{4,3,2,1,0:T(8,128)} pad(f32[2,2,2,128,128]{4,3,2,1,0:T(8,128)} %pad_maximum_fusion.4, f32[]{:T(128)} %constant.23.clone.1), padding=0_0_0x0_0_0x0_1_1x0_0_0x0_0_0 | pad | bytes 1572868 | tf_op jit(solution)/shard_map/pad | solution.py:181
  241.7 5.7 %pad.48 = f32[2,2,4,128,128]{4,3,2,1,0:T(8,128)} pad(f32[2,2,2,128,128]{4,3,2,1,0:T(8,128)} %pad_add_fusion.1, f32[]{:T(128)} %constant.23.clone.1), padding=0_0_0x0_0_0x1_0_1x0_0_0x0_0_0 | pad | bytes 1572868 | tf_op jit(solution)/shard_map/pad | solution.py:181
  252.0 10.2 %pad.121 = f32[2,2,8,128,128]{4,3,2,1,0:T(8,128)} pad(f32[2,2,4,128,128]{4,3,2,1,0:T(8,128)} %add.201, f32[]{:T(128)} %constant.23.clone.1), padding=0_0_0x0_0_0x1_0_1x0_0_0x0_0_0 | pad | bytes 3145732
  264.4 10.2 %pad.49 = f32[2,2,8,128,128]{4,3,2,1,0:T(8,128)} pad(f32[2,2,4,128,128]{4,3,2,1,0:T(8,128)} %pad_maximum_fusion.2, f32[]{:T(128)} %constant.23.clone.1), padding=0_0_0x0_0_0x0_1_1x0_0_0x0_0_0 | pad | bytes 3145732 | tf_op jit(solution)/shard_map/pad | solution.py:181
  279.4 3.7 pad.41
  289.4 6.3 %pad.123 = f32[2,2,7,128,128]{4,3,2,1,0:T(8,128)} pad(f32[2,2,4,128,128]{4,3,2,1,0:T(8,128)S(1)} %add.194, f32[]{:T(128)} %constant.23.clone.1), padding=0_0_0x0_0_0x0_0_1x0_0_0x0_0_0 | pad | bytes 2883588
  297.4 10.1 %pad.70 = f32[2,2,7,128,128]{4,3,2,1,0:T(8,128)} pad(f32[2,2,4,128,128]{4,3,2,1,0:T(8,128)} %pad_maximum_fusion.2, f32[]{:T(128)} %constant.23.clone.1), padding=0_0_0x0_0_0x0_0_1x0_0_0x0_0_0 | pad | bytes 2883588 | tf_op jit(solution)/shard_map/slice | solution.py:188
  307.5 6.4 %pad.44 = f32[2,2,8,128,128]{4,3,2,1,0:T(8,128)} pad(f32[2,2,4,128,128]{4,3,2,1,0:T(8,128)S(1)} %add.194, f32[]{:T(128)} %constant.23.clone.1), padding=0_0_0x0_0_0x1_0_1x0_0_0x0_0_0 | pad | bytes 3145732 | tf_op jit(solution)/shard_map/pad | solution.py:181
  316.3 6.4 %pad.43 = f32[2,2,8,128,128]{4,3,2,1,0:T(8,128)} pad(f32[2,2,4,128,128]{4,3,2,1,0:T(8,128)S(1)} %pad_maximum_fusion.1, f32[]{:T(128)} %constant.23.clone.1), padding=0_0_0x0_0_0x0_1_1x0_0_0x0_0_0 | pad | bytes 3145732 | tf_op jit(solution)/shard_map/pad | solution.py:181
  328.7 4.7 %fusion.13 = f32[2,2,8,128,128]{4,3,2,1,0:T(8,128)S(1)} fusion(f32[2,2,8,128,128]{4,2,3,1,0:T(8,128)S(1)} %copy-done.12, f32[2,2,8,128,128]{4,2,3,1,0:T(8,128)S(1)} %copy-done.8), kind=kOutput, calls=%fused_computation.20 | convolution fusion | flops 805306368 | bytes 6291456 | tf_op jit(solution)/shard_map/...ik,...jk->...ij/dot_general | solution.py:97
  333.5 8.9 %while.12 = (s32[]{:T(128)}, f32[2,2,128,128]{3,2,1,0:T(8,128)S(1)}, s32[]{:T(128)}, f32[8,2,2,128,128]{4,3,2,1,0:T(8,128)}, f32[8,2,2,128,128]{4,3,2,1,0:T(8,128)}, /*index=5*/s32[]{:T(128)}, s32[]{:T(128)}, s32[]{:T(128)}) while((s32[]{:T(128)}, f32[2,2,128,128]{3,2,1,0:T(8,128)S(1)}, s32[]{:T(128)}, f32[8,2,2,128,128]{4,3,2,1,0:T(8,128)}, ...), condition=%wide.region_5.6_spmd, body=%wide.region_4.5_spmd.sunk | while | flops 100728832 | bytes 1574015 | solution.py:55
  342.4 4.1 %pad_add_fusion = f32[2,2,8,128,128]{4,3,2,1,0:T(8,128)S(1)} fusion(f32[2,2,7,128,128]{4,3,2,1,0:T(8,128)} %slice_add_fusion.2, f32[2,2,7,128,128]{4,3,2,1,0:T(8,128)} %slice_add_fusion, f32[2,2,1,128,128]{4,3,2,1,0:T(8,128)S(1)} %broadcast_in_dim.86, f32[2,2,128,128]{3,2,1,0:T(8,128)S(1)} %get-tuple-element.49), kind=kOutput, calls=%fused_computation.37 | convolution fusion | flops 806354944 | bytes 6291456 | tf_op jit(solution)/shard_map/dot_general | solution.py:59
  355.4 22.5 %all_to_all.44 = bf16[2,1024,256]{2,0,1:T(2,128)(2,1)S(1)} all-to-all(bf16[2,1024,256]{2,0,1:T(2,128)(2,1)S(1)} %reshape.170), channel_id=1, replica_groups=mesh['head'=16,'seq'=8] {'head'}, dimensions={1} | all-to-all | bytes 2097152 | tf_op jit(solution)/shard_map/all_to_all | solution.py:197
  387.9 3.6 multiply_convert_fusion
  (177 shorter events, 138.9 us)
Async XLA Ops:
  6.5 74.1 %copy-start = (bf16[128,4096]{1,0:T(8,128)(2,1)S(1)}, bf16[128,4096]{1,0:T(8,128)(2,1)}, u32[]{:S(2)}) copy-start(bf16[128,4096]{1,0:T(8,128)(2,1)} %param.19) | copy-start | bytes 3145732
  6.5 33.0 %copy-start.19 = (bf16[2,64,4096]{2,1,0:T(8,128)(2,1)S(1)}, bf16[2,64,4096]{2,1,0:T(8,128)(2,1)}, u32[]{:S(2)}) copy-start(bf16[2,64,4096]{2,1,0:T(8,128)(2,1)} %param.16) | copy-start | bytes 3145732
  8.1 15.6 %all-to-all-start.3 = ((bf16[16,2,128]{2,1,0:T(2,128)(2,1)}), bf16[16,2,128]{2,1,0:T(2,128)(2,1)S(1)}, u32[]{:S(2)}, u32[]{:S(2)}) async-start(bf16[16,2,128]{2,1,0:T(2,128)(2,1)} %reshape.176), calls=%async_computation.3 | async-start | bytes 16384 | tf_op jit(solution)/shard_map/all_to_all | solution.py:133
  35.9 30.0 %all-to-all-start.1 = ((bf16[16,2,64,128]{3,2,1,0:T(8,128)(2,1)}), bf16[16,2,64,128]{3,2,1,0:T(8,128)(2,1)S(1)}, u32[]{:S(2)}, u32[]{:S(2)}) async-start(bf16[16,2,64,128]{3,2,1,0:T(8,128)(2,1)} %broadcast_in_dim.40), calls=%async_computation.1 | async-start | bytes 1048576 | tf_op jit(solution)/shard_map/all_to_all | solution.py:31
  65.9 7.6 %copy-start.23 = (f32[32]{0:T(128)S(1)}, f32[32]{0:T(128)}, u32[]{:S(2)}) copy-start(f32[32]{0:T(128)} %param.21) | copy-start | bytes 388
  65.9 45.4 %all-to-all-start = ((bf16[16,2,49152]{2,1,0:T(2,128)(2,1)}), bf16[16,2,49152]{2,1,0:T(2,128)(2,1)}, u32[]{:S(2)}, u32[]{:S(2)}) async-start(bf16[16,2,49152]{2,1,0:T(2,128)(2,1)} %reshape.174), calls=%async_computation | async-start | bytes 6291456 | tf_op jit(solution)/shard_map/all_to_all | solution.py:19
  73.2 260.2 %all-gather.7.cloned.1.call-start = ((), (), s32[]{:S(2)}) async-start(), calls=%async_computation.6 | async-start | bytes 2359296 | tf_op jit(solution)/shard_map/all_gather | solution.py:47
  133.5 4.3 %copy-start.2 = (bf16[6,64,16,256]{3,1,2,0:T(8,128)(2,1)S(1)}, bf16[6,64,16,256]{3,1,2,0:T(8,128)(2,1)}, u32[]{:S(2)}) copy-start(bf16[6,64,16,256]{3,1,2,0:T(8,128)(2,1)} %copy.164) | copy-start | bytes 9437188
  171.5 8.1 %copy-start.20 = (f32[2,8,128,2]{2,1,3,0:T(8,128)S(1)}, f32[2,8,128,2]{2,1,3,0:T(8,128)}, u32[]{:S(2)}) copy-start(f32[2,8,128,2]{2,1,3,0:T(8,128)} %reshape.160) | copy-start | bytes 49156
  179.6 4.8 %copy-start.7 = (f32[2,2,8,128,128]{4,2,3,1,0:T(8,128)}, f32[2,2,8,128,128]{4,2,3,1,0:T(8,128)S(1)}, u32[]{:S(2)}) copy-start(f32[2,2,8,128,128]{4,2,3,1,0:T(8,128)S(1)} %get-tuple-element.65) | copy-start | bytes 6291460
  220.2 4.6 %copy-start.5 = (f32[2,2,8,128,128]{3,4,2,1,0:T(8,128)}, f32[2,2,8,128,128]{3,4,2,1,0:T(8,128)S(1)}, u32[]{:S(2)}) copy-start(f32[2,2,8,128,128]{3,4,2,1,0:T(8,128)S(1)} %copy.182) | copy-start | bytes 6291460
  220.2 4.6 %copy-start.3 = (f32[2,2,8,128,128]{4,3,2,1,0:T(8,128)S(1)}, f32[2,2,8,128,128]{4,3,2,1,0:T(8,128)}, u32[]{:S(2)}) copy-start(f32[2,2,8,128,128]{4,3,2,1,0:T(8,128)} %fusion.17) | copy-start | bytes 6291460
  220.2 4.6 %copy-start.21 = (f32[2,2,8,128]{3,2,1,0:T(8,128)S(1)}, f32[2,2,8,128]{3,2,1,0:T(8,128)}, u32[]{:S(2)}) copy-start(f32[2,2,8,128]{3,2,1,0:T(8,128)} %exponential_multiply_fusion) | copy-start | bytes 49156
  224.8 5.9 %copy-start.9 = (f32[2,2,8,128,128]{4,3,2,1,0:T(8,128)}, f32[2,2,8,128,128]{4,3,2,1,0:T(8,128)S(1)}, u32[]{:S(2)}) copy-start(f32[2,2,8,128,128]{4,3,2,1,0:T(8,128)S(1)} %fusion.136) | copy-start | bytes 6291460
  232.6 1.6 copy-start.17
  247.4 3.6 copy-start.13
  247.4 3.6 copy-start.14
  252.0 10.2 %slice-start = ((f32[2,2,8,128,128]{4,3,2,1,0:T(8,128)}), f32[2,2,1,128,128]{4,3,2,1,0:T(8,128)S(1)}, s32[]{:S(2)}) async-start(f32[2,2,8,128,128]{4,3,2,1,0:T(8,128)} %copy-done.9), calls=%async_computation.7 | async-start | bytes 524288 | tf_op jit(solution)/shard_map/slice | solution.py:181
  276.4 57.1 %all-gather.5.cloned.1.call-start = ((), (), s32[]{:S(2)}) async-start(), calls=%async_computation.5 | async-start | bytes 2359296 | tf_op jit(solution)/shard_map/all_gather | solution.py:47
  277.4 1.9 copy-start.18
  316.3 6.4 %copy-start.10 = (f32[2,2,8,128,128]{4,3,2,1,0:T(8,128)S(1)}, f32[2,2,8,128,128]{4,3,2,1,0:T(8,128)}, u32[]{:S(2)}) copy-start(f32[2,2,8,128,128]{4,3,2,1,0:T(8,128)} %pad.121) | copy-start | bytes 6291460
  322.7 3.1 copy-start.15
  322.7 3.1 copy-start.16
  325.8 2.3 copy-start.8
  325.8 2.9 copy-start.12
  342.4 4.1 %copy-start.4 = (f32[2,2,8,128,128]{4,3,2,1,0:T(8,128)S(1)}, f32[2,2,8,128,128]{4,3,2,1,0:T(8,128)}, u32[]{:S(2)}) copy-start(f32[2,2,8,128,128]{4,3,2,1,0:T(8,128)} %fusion.17) | copy-start | bytes 6291460
  346.5 2.2 copy-start.6
  348.7 2.4 copy-start.11
  385.2 2.7 copy-start.22
  387.9 3.6 copy-start.1
Sparse Core Ops, SparseCore 0:
  276.5 23.6 all-gather.6
  301.9 25.6 all-gather.4
where the time goes:
time: 406 us; the launch traced here: 399 us
  local copies, waits for them, and re-layouts  161 us (40%)
  matrix products  84.5 us (21%)
  other arithmetic  55.9 us (14%)
  blocking collectives  33.1 us (8%)
  waiting for transfers between devices  30.7 us (8%)
  starting transfers between devices  19.2 us (5%)
  between operations  14.4 us (4%)
    dot_general x34, matrix products, product(): return jnp.matmul(left_side, right_side, precision=exact_mode)  65.3 us
    unnamed x58, local copies, waits for them, and re-layouts  46.7 us
    pad x7, local copies, waits for them, and re-layouts, per_device(): inclusive = lax.associative_scan(compose, (move_mats, offsets), axis=2)  41.8 us
    all_to_all x1, waiting for transfers between devices, in_one_piece(): lax.all_to_all(both, axis, split_axis=split_dim, concat_axis=concat_dim,...  23.9 us
    all_to_all x1, blocking collectives, per_device(): lax.all_to_all(core_rows, 'head', split_axis=1, concat_axis=2, tiled=True)  22.5 us
    add x7, other arithmetic, per_device(): inclusive = lax.associative_scan(compose, (move_mats, offsets), axis=2)  10.9 us
    all_to_all x1, blocking collectives, copy_for_each(): return lax.all_to_all(copies, axis, split_axis=0, concat_axis=0, tiled=True)  10.6 us
    slice x1, local copies, waits for them, and re-layouts, per_device(): inclusive[1][:, :, :-1]  10.1 us
  transfers between devices with their start and end apart: 5, of which 2 were waited for; matrix products, arithmetic and copies ran while one was open for 24% of the time, Pallas kernels for 0%

commit v1 on v0

v1 whole, which is shorter than its diff:
```python
import functools

import jax
import jax.numpy as jnp
from jax import lax
from jax.experimental import pallas as pl
from jax.experimental.pallas import tpu as pltpu
from jax.sharding import PartitionSpec as P

H = 32
DK = 128
TOK = 64
C = 128
SPAN = 2048
GROUPS = 16
OWNERS = 32
NORM_EPS = 1e-6
MESH = pl.DeviceIdType.MESH
F32 = jnp.float32
BF16 = jnp.bfloat16
ANY = pl.BlockSpec(memory_space=pl.ANY)
VM = pl.BlockSpec(memory_space=pltpu.VMEM)


def place():
    group = lax.axis_index("head")
    seq = lax.axis_index("seq")
    core = lax.rem(seq, 2)
    return group, seq, core, group * 2 + core, core * GROUPS + group


def owner_id(owner, seq, core):
    return {"head": owner // 2, "seq": seq - core + lax.rem(owner, 2)}


def greet(seq, core, me):
    barrier = pltpu.get_barrier_semaphore()

    def one(step, carry):
        other = lax.rem(me + step, OWNERS)
        pl.semaphore_signal(
            barrier, inc=1, device_id=owner_id(other, seq, core), device_id_type=MESH
        )
        return carry

    lax.fori_loop(1, OWNERS, one, 0)
    return barrier


def entry_kernel(
    q_in, k_in, v_in, lat_in, aux_in, q_out, k_out, v_out, lat_out, aux_out, send, recv
):
    group, seq, core, me, blk = place()
    barrier = greet(seq, core, me)
    pl.semaphore_wait(barrier, OWNERS - 1)
    rows = pl.ds(pl.multiple_of(blk * TOK, TOK), TOK)

    def lat_send(step, carry):
        other = lax.rem(group + step, GROUPS)
        pltpu.make_async_remote_copy(
            lat_in, lat_out.at[:, rows, :], send.at[3], recv.at[3],
            device_id={"head": other, "seq": seq}, device_id_type=MESH,
        ).start()
        return carry

    lax.fori_loop(1, GROUPS, lat_send, 0)
    pltpu.make_async_copy(lat_in, lat_out.at[:, rows, :], recv.at[3]).start()

    def aux_send(step, carry):
        other = lax.rem(me + step, OWNERS)
        pltpu.make_async_remote_copy(
            aux_in.at[other], aux_out.at[blk], send.at[4], recv.at[4],
            device_id=owner_id(other, seq, core), device_id_type=MESH,
        ).start()
        return carry

    lax.fori_loop(1, OWNERS, aux_send, 0)
    pltpu.make_async_copy(aux_in.at[me], aux_out.at[blk], recv.at[4]).start()

    for slot, src, dst in ((0, k_in, k_out), (1, v_in, v_out), (2, q_in, q_out)):

        def piece_send(step, carry, slot=slot, src=src, dst=dst):
            other = lax.rem(me + step, OWNERS)
            cols = pl.ds(pl.multiple_of(other * DK, DK), DK)
            pltpu.make_async_remote_copy(
                src.at[:, :, cols], dst.at[:, rows, :], send.at[slot], recv.at[slot],
                device_id=owner_id(other, seq, core), device_id_type=MESH,
            ).start()
            return carry

        lax.fori_loop(1, OWNERS, piece_send, 0)
        own = pl.ds(pl.multiple_of(me * DK, DK), DK)
        pltpu.make_async_copy(src.at[:, :, own], dst.at[:, rows, :], recv.at[slot]).start()

    half = pl.ds(pl.multiple_of(core * 1024, 1024), 1024)
    mine = lat_out.at[:, half, :]
    pltpu.make_async_copy(mine, mine, recv.at[3]).wait()
    pass_on = pltpu.make_async_remote_copy(
        mine, mine, send.at[5], recv.at[5],
        device_id={"seq": seq + 1 - 2 * core}, device_id_type=MESH,
    )
    pass_on.start()
    for slot, dst in ((4, aux_out), (0, k_out), (1, v_out), (2, q_out)):
        pltpu.make_async_copy(dst, dst, recv.at[slot]).wait()
    pass_on.wait()
    sent = k_in.at[:, :, pl.ds(0, (OWNERS - 1) * DK)]
    for slot in (0, 1, 2):
        pltpu.make_async_copy(sent, sent, send.at[slot]).wait()
    lat_sent = lat_out.at[:, pl.ds(0, (GROUPS - 1) * TOK), :]
    pltpu.make_async_copy(lat_sent, lat_sent, send.at[3]).wait()
    aux_sent = aux_in.at[pl.ds(0, OWNERS - 1)]
    pltpu.make_async_copy(aux_sent, aux_sent, send.at[4]).wait()


def entry_exchange(q, k, v, lat, aux):
    wide = jax.ShapeDtypeStruct((2, SPAN, DK), BF16)
    return pl.pallas_call(
        entry_kernel,
        out_shape=(wide, wide, wide, wide, jax.ShapeDtypeStruct((OWNERS, 8, 128), BF16)),
        in_specs=[ANY] * 5,
        out_specs=(ANY,) * 5,
        scratch_shapes=[pltpu.SemaphoreType.DMA((6,)), pltpu.SemaphoreType.DMA((6,))],
        compiler_params=pltpu.CompilerParams(collective_id=0, has_side_effects=True),
        name="entry_exchange",
    )(q, k, v, lat, aux)


def halves(x):
    high = x.astype(BF16)
    return high, (x - high.astype(F32)).astype(BF16)


def fine_dot(left, right):
    lh, ll = halves(left)
    rh, rl = halves(right)
    return jnp.dot(
        jnp.concatenate([lh, ll, lh], axis=1),
        jnp.concatenate([rh, rh, rl], axis=0),
        preferred_element_type=F32,
    )


def fine_dot_nt(left, right):
    lh, ll = halves(left)
    rh, rl = halves(right)
    return lax.dot_general(
        jnp.concatenate([lh, ll, lh], axis=1),
        jnp.concatenate([rh, rh, rl], axis=1),
        (((1,), (1,)), ((), ())),
        preferred_element_type=F32,
    )


def softplus(x):
    u = jnp.exp(-jnp.abs(x))
    series = u * (1.0 - u * (0.5 - u * (1.0 / 3.0 - u * 0.25)))
    return jnp.maximum(x, 0.0) + jnp.where(u < 0.015625, series, jnp.log(1.0 + u))


def unit(x):
    x = x.astype(F32)
    return x * lax.rsqrt(jnp.sum(x * x, axis=-1, keepdims=True) + NORM_EPS)


def local_kernel(
    pairs, q_ref, k_ref, v_ref, lat_ref, aux_ref, up_ref, bias_ref, rate_ref,
    ol_ref, rh_ref, rl_ref, map_ref, state,
):
    step = pl.program_id(0)

    ri = lax.broadcasted_iota(jnp.int32, (C, C), 0)
    ci = lax.broadcasted_iota(jnp.int32, (C, C), 1)
    eye = ri == ci
    strict = ri > ci
    lower = ri >= ci
    tri = lower.astype(BF16)
    tri2 = jnp.concatenate([tri, tri], axis=1)
    upper = (ri <= ci).astype(BF16)
    up = up_ref[...]
    bias0 = bias_ref[0:1, :]
    bias1 = bias_ref[1:2, :]
    rate = -jnp.exp(rate_ref[...])

    @pl.when(step == 0)
    def _():
        state[...] = jnp.zeros_like(state)
        for chain in range(2):
            state[chain, :, 0:C] = eye.astype(F32)

    todo = []
    for j in range(pairs):
        rows = aux_ref[2 * j].astype(F32) + aux_ref[2 * j + 1].astype(F32)
        counts = jnp.dot(rows.astype(BF16), upper, preferred_element_type=F32)
        both = jnp.concatenate([jax.nn.sigmoid(rows), counts, rows], axis=0)
        both = jnp.concatenate([both, jnp.zeros((C - 24, C), F32)], axis=0)
        cols = both.T
        for chain in range(2):
            todo.append(
                dict(
                    j=j, chain=chain,
                    beta=cols[:, chain:chain + 1],
                    count_col=cols[:, 10 + chain:11 + chain],
                    kind=cols[:, 20 + chain:21 + chain],
                    count_row=counts[2 + chain:3 + chain, :],
                    count_last=counts[2 + chain:3 + chain, C - 1:C],
                )
            )
    for t in todo:
        at = pl.ds(t["j"] * C, C)
        chain = t["chain"]
        pre = jnp.dot(lat_ref[chain, at, :], up, preferred_element_type=F32)
        pre = pre.astype(BF16).astype(F32)
        bias = jnp.where(t["kind"] > 0.5, bias1, bias0)
        decay = rate * softplus(pre + bias)
        dh, dl = halves(decay)
        total = jnp.dot(tri2, jnp.concatenate([dh, dl], axis=0), preferred_element_type=F32)
        t["total"] = total
        t["growth"] = jnp.exp(total)
    for t in todo:
        at = pl.ds(t["j"] * C, C)
        chain = t["chain"]
        total, growth = t["total"], t["growth"]
        key = unit(k_ref[chain, at, :])
        query = unit(q_ref[chain, at, :]) * (DK ** -0.5)
        t["alive"] = (t["count_col"] < 0.5).astype(F32)
        same = t["count_col"] == t["count_row"]
        last = total[C - 1:C, :]
        key_grow = key * growth
        query_grow = query * growth
        key_shrink = key * jnp.exp(-total)
        tail_mask = (t["count_col"] == t["count_last"]).astype(F32)
        t["tail"] = key * jnp.exp(last - total) * tail_mask
        t["carry"] = jnp.exp(last) * (t["count_last"] < 0.5).astype(F32)
        gram = fine_dot_nt(jnp.concatenate([key_grow, query_grow], axis=0), key_shrink)
        t["mix"] = jnp.where(lower & same, gram[C:], 0.0)
        t["low"] = jnp.where(strict & same, gram[:C], 0.0) * t["beta"]
        t["query_live"] = query_grow * t["alive"]
        t["rhs"] = jnp.concatenate(
            [key_grow * (t["alive"] * t["beta"]), v_ref[chain, at, :].astype(F32) * t["beta"]],
            axis=1,
        )

    near = (ri // 16) == (ci // 16)
    for t in todo:
        t["d"] = jnp.where(near, t["low"], 0.0)
    for t in todo:
        t["d2"] = fine_dot(t["d"], t["d"])
    for t in todo:
        both = fine_dot(jnp.concatenate([t["d"], t["d2"]], axis=0), t["d2"])
        t["x"] = t["d2"] - t["d"] - both[:C]
        t["d4"] = both[C:]
    for t in todo:
        both = fine_dot(jnp.concatenate([t["x"], t["d4"]], axis=0), t["d4"])
        t["x"] = t["x"] + t["d4"] + both[:C]
        t["d8"] = both[C:]
    for t in todo:
        t["x"] = t["x"] + t["d8"] + fine_dot(t["x"], t["d8"])
    width = 16
    while width < C:
        part = ((ri // (2 * width)) == (ci // (2 * width))) & ((ri // width) != (ci // width))
        for t in todo:
            off = jnp.where(part, t["low"], 0.0)
            t["y"] = off + fine_dot(off, t["x"])
        for t in todo:
            t["x"] = t["x"] - (t["y"] + fine_dot(t["x"], t["y"]))
        width *= 2

    for t in todo:
        t["wu"] = t["rhs"] + fine_dot(t["x"], t["rhs"])
    for t in todo:
        wh, wl = halves(t["wu"])
        right = jnp.concatenate([wh, wh, wl], axis=0)
        mh, ml = halves(t["mix"])
        kh, kl = halves(t["tail"].T)
        left = jnp.concatenate(
            [jnp.concatenate([mh, ml, mh], axis=1), jnp.concatenate([kh, kl, kh], axis=1)], axis=0
        )
        both = jnp.dot(left, right, preferred_element_type=F32)
        t["pu"] = both[:C, C:]
        live = t["query_live"] - both[:C, :C]
        move = jnp.where(eye, t["carry"], 0.0) - both[C:, :C]
        t["left"] = jnp.concatenate([live, move], axis=0)
        t["offset"] = both[C:, C:]
    held = [state[0], state[1]]
    for t in todo:
        at = pl.ds(t["j"] * C, C)
        chain = t["chain"]
        both = fine_dot(t["left"], held[chain])
        ol_ref[chain, at, :] = t["pu"] + both[:C, C:]
        high, low = halves(both[:C, :C])
        rh_ref[chain, at, :] = high
        rl_ref[chain, at, :] = low
        held[chain] = jnp.concatenate([both[C:, :C], both[C:, C:] + t["offset"]], axis=1)
    state[0] = held[0]
    state[1] = held[1]
    map_ref[0] = held[0]
    map_ref[1] = held[1]


def local_work(q, k, v, lat, aux, up, bias, rate, pairs=2):
    steps = SPAN // (pairs * C)
    wide = pl.BlockSpec((2, pairs * C, DK), lambda i: (0, i, 0))
    whole = lambda *shape: pl.BlockSpec(shape, lambda i: (0,) * len(shape))
    return pl.pallas_call(
        functools.partial(local_kernel, pairs),
        grid=(steps,),
        out_shape=(
            jax.ShapeDtypeStruct((2, SPAN, DK), F32),
            jax.ShapeDtypeStruct((2, SPAN, DK), BF16),
            jax.ShapeDtypeStruct((2, SPAN, DK), BF16),
            jax.ShapeDtypeStruct((2, DK, 2 * DK), F32),
        ),
        in_specs=[
            wide, wide, wide, wide,
            pl.BlockSpec((2 * pairs, 8, 128), lambda i: (i, 0, 0)),
            whole(DK, DK), whole(2, DK), whole(1, DK),
        ],
        out_specs=(wide, wide, wide, whole(2, DK, 2 * DK)),
        scratch_shapes=[pltpu.VMEM((2, DK, 2 * DK), F32)],
        name="local_work",
    )(q, k, v, lat, aux, up, bias, rate)


def exit_kernel(
    ol_ref, rh_ref, rl_ref, map_ref, back_ref,
    first, second, moved, core_buf, sem_send, sem_recv, back_send, back_recv,
):
    group, seq, core, me, blk = place()
    x = seq // 2
    barrier = greet(seq, core, me)
    for away in (1, 2, 3):
        pl.semaphore_signal(
            barrier, inc=1, device_id={"seq": lax.rem(seq + 2 * away, 8)}, device_id_type=MESH
        )
    pl.semaphore_wait(barrier, OWNERS + 2)

    def send_to(src, dst, slot, to):
        return pltpu.make_async_remote_copy(
            src, dst, sem_send.at[slot], sem_recv.at[slot],
            device_id={"seq": 2 * to + core}, device_id_type=MESH,
        )

    for chain in range(2):
        moved[chain] = map_ref[chain, :, DK:]

    @pl.when(x == 0)
    def _():
        first[...] = jnp.zeros_like(first)
        send_to(moved, first, 0, 1).start()
        send_to(moved, first, 0, 1).wait_send()

    @pl.when(x == 2)
    def _():
        send_to(map_ref, second, 1, 3).start()

    @pl.when(x == 1)
    def _():
        send_to(moved, first, 0, 1).wait_recv()
        for chain in range(2):
            moved[chain] = map_ref[chain, :, DK:] + fine_dot(map_ref[chain, :, 0:DK], first[chain])
        send_to(moved, first, 0, 2).start()
        send_to(moved, first, 2, 3).start()
        send_to(moved, first, 0, 2).wait_send()
        send_to(moved, first, 2, 3).wait_send()

    @pl.when(x == 2)
    def _():
        send_to(map_ref, second, 1, 3).wait_send()
        send_to(moved, first, 0, 2).wait_recv()

    @pl.when(x == 3)
    def _():
        send_to(map_ref, second, 1, 3).wait_recv()
        send_to(moved, first, 2, 3).wait_recv()
        for chain in range(2):
            first[chain] = second[chain, :, DK:] + fine_dot(second[chain, :, 0:DK], first[chain])

    rights = []
    for chain in range(2):
        sh, sl = halves(first[chain])
        rights.append(jnp.concatenate([sh, sh, sl], axis=0))

    mine = pl.ds(pl.multiple_of(me * DK, DK), DK)

    def piece(step, carry):
        j = lax.rem(step + group, SPAN // C)
        at = pl.ds(pl.multiple_of(j * C, C), C)
        for chain in range(2):
            high = rh_ref[chain, at, :]
            left = jnp.concatenate([high, rl_ref[chain, at, :], high], axis=1)
            out = ol_ref[chain, at, :] + jnp.dot(left, rights[chain], preferred_element_type=F32)
            core_buf[chain, at, :] = out.astype(BF16)
        for part in range(2):
            b = 2 * j + part
            rows = pl.ds(pl.multiple_of(b * TOK, TOK), TOK)

            @pl.when(b != blk)
            def _():
                pltpu.make_async_remote_copy(
                    core_buf.at[:, rows, :], back_ref.at[:, :, mine], back_send, back_recv,
                    device_id={"head": lax.rem(b, GROUPS), "seq": seq - core + b // GROUPS},
                    device_id_type=MESH,
                ).start()

            @pl.when(b == blk)
            def _():
                pltpu.make_async_copy(
                    core_buf.at[:, rows, :], back_ref.at[:, :, mine], back_recv
                ).start()
        return carry

    lax.fori_loop(0, SPAN // C, piece, 0)
    pltpu.make_async_copy(back_ref, back_ref, back_recv).wait()
    sent = back_ref.at[:, :, pl.ds(0, (OWNERS - 1) * DK)]
    pltpu.make_async_copy(sent, sent, back_send).wait()


def exit_exchange(ol, rh, rl, maps):
    return pl.pallas_call(
        exit_kernel,
        out_shape=jax.ShapeDtypeStruct((2, TOK, H * DK), BF16),
        in_specs=[VM] * 4,
        out_specs=ANY,
        scratch_shapes=[
            pltpu.VMEM((2, DK, DK), F32),
            pltpu.VMEM((2, DK, 2 * DK), F32),
            pltpu.VMEM((2, DK, DK), F32),
            pltpu.VMEM((2, SPAN, DK), BF16),
            pltpu.SemaphoreType.DMA((3,)),
            pltpu.SemaphoreType.DMA((3,)),
            pltpu.SemaphoreType.DMA,
            pltpu.SemaphoreType.DMA,
        ],
        compiler_params=pltpu.CompilerParams(collective_id=1, has_side_effects=True),
        name="exit_exchange",
    )(ol, rh, rl, maps)


def gate_kernel(core_ref, gate_ref, gain_ref, out_ref):
    for b in range(2):
        for h in range(core_ref.shape[2] // DK):
            cols = slice(h * DK, (h + 1) * DK)
            wide = core_ref[b, :, cols].astype(F32)
            norm = lax.rsqrt(jnp.mean(wide * wide, axis=-1, keepdims=True) + NORM_EPS)
            gate = jax.nn.sigmoid(gate_ref[b, :, cols].astype(F32))
            out_ref[b, :, cols] = (wide * norm * gain_ref[0:1, cols] * gate).astype(BF16)


def norm_gate(core, gate, gain):
    width = 1024
    spec = pl.BlockSpec((2, TOK, width), lambda i: (0, 0, i))
    return pl.pallas_call(
        gate_kernel,
        grid=(H * DK // width,),
        out_shape=jax.ShapeDtypeStruct(core.shape, BF16),
        in_specs=[spec, spec, pl.BlockSpec((1, width), lambda i: (0, i))],
        out_specs=spec,
        name="norm_gate",
    )(core, gate, gain.reshape(1, -1))


def pack_small(beta_raw, boundary, modality):
    core_group = lax.axis_index("head")
    beta = beta_raw.astype(F32).transpose(2, 0, 1)
    mark = jnp.broadcast_to(boundary.astype(F32)[None], (OWNERS, 2, TOK))
    kind = jnp.broadcast_to(modality.astype(F32)[None], (OWNERS, 2, TOK))
    rows = jnp.concatenate([beta, mark, kind, jnp.zeros((OWNERS, 2, TOK), F32)], axis=1)
    odd = (lax.rem(core_group, 2) == 1).astype(F32)
    return jnp.concatenate([rows * (1.0 - odd), rows * odd], axis=2).astype(BF16)


def per_device(
    query_rows, key_rows, value_rows, beta_raw, gate_latent, gate_up, dt_bias, decay_log,
    boundary, modality, out_gate, norm_gain,
):
    me = lax.axis_index("head") * 2 + lax.rem(lax.axis_index("seq"), 2)
    aux = pack_small(beta_raw, boundary, modality)
    q, k, v, lat, aux = entry_exchange(query_rows, key_rows, value_rows, gate_latent, aux)
    up = lax.dynamic_slice_in_dim(gate_up, me * DK, DK, 1)
    bias = lax.dynamic_slice_in_dim(dt_bias, me * DK, DK, 1)
    rate = jnp.broadcast_to(lax.dynamic_slice_in_dim(decay_log, me, 1, 0)[None], (1, DK))
    ol, rh, rl, maps = local_work(q, k, v, lat, aux, up, bias, rate)
    back = exit_exchange(ol, rh, rl, maps)
    return norm_gate(back, out_gate, norm_gain)


def solution(mesh):
    rows = P(None, ("seq", "head"), None)
    flat = P(None, ("seq", "head"))
    return jax.shard_map(
        per_device,
        mesh=mesh,
        in_specs=(rows, rows, rows, rows, rows, P(), P(), P(), flat, flat, rows, P()),
        out_specs=rows,
        check_vma=False,
    )
```

time: 406 us -> 131 us (0.32)
  the two profiles are of different devices: /device:TPU:6 before, /device:TPU:7 now
where the time goes in v1:
time: 131 us
  Pallas kernels  123 us (94%)
  local copies, waits for them, and re-layouts  5.25 us (4%)
  other arithmetic  2.19 us (2%)
    pallas_call x1, Pallas kernels, entry_exchange(): pl.pallas_call(entry_kernel, out_shape=(wide, wide, wide, wide, jax.Shape...  54 us
    pallas_call x1, Pallas kernels, local_work(): pl.pallas_call(functools.partial(local_kernel, pairs), grid=(steps,), out...  34 us
    pallas_call x1, Pallas kernels, exit_exchange(): pl.pallas_call(exit_kernel, out_shape=jax.ShapeDtypeStruct((2, TOK, H * D...  31.3 us
    pallas_call x1, Pallas kernels, norm_gate(): pl.pallas_call(gate_kernel, grid=(H * DK // width,), out_shape=jax.ShapeD...  4 us

profile of v1, /device:TPU:7, one launch (start us, length us, event | category | flops | bytes accessed | tf_op | source)
XLA Modules:
  0.0 130.7 jit_solution(14612562175171733376)
XLA Ops:
  0.0 0.0 copy-start
  0.0 1.3 %dynamic_slice.11 = f32[1]{0:T(128)} dynamic-slice(f32[32]{0:T(128)} %param.19, s32[]{:T(128)S(6)} %select_n.8), dynamic_slice_sizes={1} | dynamic-slice | bytes 12 | tf_op jit(solution)/shard_map/dynamic_slice | solution.py:481
  1.3 1.2 broadcast_in_dim.27.rate_ref
  2.6 0.1 pad.5.clone
  2.6 1.3 constant_dynamic-slice_fusion.bias_ref
  3.9 0.7 convert_element_type.11
  4.6 0.7 convert_element_type.12
  5.3 0.0 copy-done
  5.3 0.6 constant_dynamic-slice_fusion.1.up_ref
  5.9 0.7 copy.16
  6.6 0.1 fusion.2
  6.7 0.7 pad_maximum_fusion.aux_in
  7.5 54.0 %entry_exchange.1 = (bf16[2,2048,128]{2,1,0:T(8,128)(2,1)}, bf16[2,2048,128]{2,1,0:T(8,128)(2,1)}, bf16[2,2048,128]{2,1,0:T(8,128)(2,1)}, bf16[2,2048,128]{2,1,0:T(8,128)(2,1)}, bf16[32,8,128]{2,1,0:T(8,128)(2,1)}) custom-call(bf16[2,64,4096]{2,1,0:T(8,128)(2,1)} %q_in.1, bf16[2,64,4096]{2,1,0:T(8,128)(2,1)} %k_in.1, bf16[2,64,4096]{2,1,0:T(8,128)(2,1)} %v_in.1, ...), custom_call_target="tpu_custom_call" | custom-call | tf_op jit(solution)/shard_map/entry_exchange/pallas_call | solution.py:117
  61.5 34.0 %local_work.1 = (f32[2,2048,128]{2,1,0:T(8,128)}, bf16[2,2048,128]{2,1,0:T(8,128)(2,1)}, bf16[2,2048,128]{2,1,0:T(8,128)(2,1)}, f32[2,128,256]{2,1,0:T(8,128)}) custom-call(bf16[2,2048,128]{2,1,0:T(8,128)(2,1)} %get-tuple-element.14.q_ref, bf16[2,2048,128]{2,1,0:T(8,128)(2,1)} %get-tuple-element.15.k_ref, bf16[2,2048,128]{2,1,0:T(8,128)(2,1)} %get-tuple-element.16.v_ref, ...), custom_call_target="tpu_custom_call" | custom-call | tf_op jit(solution)/shard_map/local_work/pallas_call | solution.py:304
  95.4 31.3 %exit_exchange.1.core_ref = bf16[2,64,4096]{2,1,0:T(8,128)(2,1)} custom-call(f32[2,2048,128]{2,1,0:T(8,128)} %get-tuple-element.19.ol_ref, bf16[2,2048,128]{2,1,0:T(8,128)(2,1)} %get-tuple-element.20.rh_ref, bf16[2,2048,128]{2,1,0:T(8,128)(2,1)} %get-tuple-element.21.rl_ref, f32[2,128,256]{2,1,0:T(8,128)} %get-tuple-element.22.map_ref), custom_call_target="tpu_custom_call" | custom-call | tf_op jit(solution)/shard_map/exit_exchange/pallas_call | solution.py:419
  126.7 4.0 %norm_gate.1 = bf16[2,64,4096]{2,1,0:T(8,128)(2,1)} custom-call(bf16[2,64,4096]{2,1,0:T(8,128)(2,1)} %exit_exchange.1.core_ref, bf16[2,64,4096]{2,1,0:T(8,128)(2,1)} %gate_ref.1, f32[1,4096]{1,0:T(1,128)} %bitcast.6), custom_call_target="tpu_custom_call" | custom-call | tf_op jit(solution)/shard_map/norm_gate/pallas_call | solution.py:452
  (3 shorter events, 0.0 us)
Async XLA Ops:
  0.0 5.3 %copy-start = (bf16[128,4096]{1,0:T(8,128)(2,1)S(1)}, bf16[128,4096]{1,0:T(8,128)(2,1)}, u32[]{:S(2)}) copy-start(bf16[128,4096]{1,0:T(8,128)(2,1)} %param.17) | copy-start | bytes 3145732

commit v2 on v0

v2 whole, which is shorter than its diff:
```python
import jax
import jax.numpy as jnp
from jax import lax
from jax.experimental import pallas as pl
from jax.experimental.pallas import tpu as pltpu
from jax.sharding import PartitionSpec as P

H = 32
DK = 128
TOK = 64
C = 128
SPAN = 2048
BLOCKS = SPAN // C
GROUPS = 16
OWNERS = 32
NORM_EPS = 1e-6
MESH = pl.DeviceIdType.MESH
F32 = jnp.float32
BF16 = jnp.bfloat16
ANY = pl.BlockSpec(memory_space=pl.ANY)
VM = pl.BlockSpec(memory_space=pltpu.VMEM)
SM = pl.BlockSpec(memory_space=pltpu.SMEM)
LAT, AUX, PASS = 6, 7, 8


def halves(x):
    high = x.astype(BF16)
    return high, (x - high.astype(F32)).astype(BF16)


def left_of(pair):
    return jnp.concatenate([pair[0], pair[1], pair[0]], axis=1)


def right_of(pair):
    return jnp.concatenate([pair[0], pair[0], pair[1]], axis=0)


def dot(left, right):
    return jnp.dot(left, right, preferred_element_type=F32)


def fine(left, right):
    return dot(left_of(left), right_of(right))


def stack(*parts):
    return jnp.concatenate(parts, axis=0)


def softplus(x):
    u = jnp.exp(-jnp.abs(x))
    series = u * (1.0 - u * (0.5 - u * (1.0 / 3.0 - u * 0.25)))
    return jnp.maximum(x, 0.0) + jnp.where(u < 0.015625, series, jnp.log(1.0 + u))


def unit(x):
    x = x.astype(F32)
    return x * lax.rsqrt(jnp.sum(x * x, axis=-1, keepdims=True) + NORM_EPS)


def aligned(start, size):
    return pl.ds(pl.multiple_of(start, size), size)


def kernel(
    q_in, k_in, v_in, beta_in, mark_in, kind_in, lat_in, up_in, bias_in, rate_in, gate_in, gain_in,
    out_ref,
    kb, vb, qb, lb, auxb, aux_src, upb, biasb, gateb, scale,
    total, grow, shrink, keyg, tail, xb, wb, ub, mcb, ocb, right, cols, rows,
    maps, first, second, moved, core_buf, back,
    send, recv, pre_send, pre_recv, back_send, back_recv, here,
):
    group = lax.axis_index("head")
    seq = lax.axis_index("seq")
    core = lax.rem(seq, 2)
    x = seq // 2
    me = group * 2 + core
    blk = core * GROUPS + group

    def owner_id(owner):
        return {"head": owner // 2, "seq": seq - core + lax.rem(owner, 2)}

    barrier = pltpu.get_barrier_semaphore()

    def greet(step, carry):
        pl.semaphore_signal(
            barrier, inc=1, device_id=owner_id(lax.rem(me + step, OWNERS)), device_id_type=MESH
        )
        return carry

    lax.fori_loop(1, OWNERS, greet, 0)
    for away in (1, 2, 3):
        pl.semaphore_signal(
            barrier, inc=1, device_id={"seq": lax.rem(seq + 2 * away, 8)}, device_id_type=MESH
        )

    my_cols = aligned(me * DK, DK)
    my_rows = aligned(blk * TOK, TOK)
    local = (
        pltpu.make_async_copy(up_in.at[:, my_cols], upb, here.at[0]),
        pltpu.make_async_copy(bias_in.at[:, my_cols], biasb, here.at[1]),
        pltpu.make_async_copy(gate_in, gateb, here.at[2]),
    )
    for copy in local:
        copy.start()

    ri = lax.broadcasted_iota(jnp.int32, (C, C), 0)
    ci = lax.broadcasted_iota(jnp.int32, (C, C), 1)
    si = lax.broadcasted_iota(jnp.int32, (8 * OWNERS, H), 0)
    sj = lax.broadcasted_iota(jnp.int32, (8 * OWNERS, H), 1)
    select = ((si % 8 == 0) & (si // 8 == sj)).astype(BF16)
    part = lax.broadcasted_iota(jnp.int32, (8 * OWNERS, TOK), 0) % 8
    ti = lax.broadcasted_iota(jnp.int32, (TOK, C), 0)
    tj = lax.broadcasted_iota(jnp.int32, (TOK, C), 1)
    packed = jnp.zeros((8 * OWNERS, C), F32)
    for b in range(2):
        small = dot(select, beta_in[b])
        small = jnp.where(part == 1, mark_in[b:b + 1, :].astype(F32), small)
        small = jnp.where(part == 2, kind_in[b:b + 1, :].astype(F32), small)
        packed = packed + dot(small.astype(BF16), (tj == ti + b * TOK).astype(BF16))
    aux_src[...] = packed.reshape(OWNERS, 8, C).astype(BF16)

    pl.semaphore_wait(barrier, OWNERS + 2)

    def lat_send(step, carry):
        pltpu.make_async_remote_copy(
            lat_in, lb.at[:, my_rows, :], send.at[LAT], recv.at[LAT],
            device_id={"head": lax.rem(group + step, GROUPS), "seq": seq}, device_id_type=MESH,
        ).start()
        return carry

    lax.fori_loop(1, GROUPS, lat_send, 0)
    pltpu.make_async_copy(lat_in, lb.at[:, my_rows, :], recv.at[LAT]).start()

    def aux_send(step, carry):
        other = lax.rem(me + step, OWNERS)
        pltpu.make_async_remote_copy(
            aux_src.at[other], auxb.at[blk], send.at[AUX], recv.at[AUX],
            device_id=owner_id(other), device_id_type=MESH,
        ).start()
        return carry

    lax.fori_loop(1, OWNERS, aux_send, 0)
    pltpu.make_async_copy(aux_src.at[me], auxb.at[blk], recv.at[AUX]).start()

    def spread(slot, src, dst, chain):
        def one(step, carry):
            other = lax.rem(me + step, OWNERS)
            pltpu.make_async_remote_copy(
                src.at[chain, :, aligned(other * DK, DK)], dst.at[chain, my_rows, :],
                send.at[slot], recv.at[slot], device_id=owner_id(other), device_id_type=MESH,
            ).start()
            return carry

        lax.fori_loop(1, OWNERS, one, 0)
        pltpu.make_async_copy(
            src.at[chain, :, my_cols], dst.at[chain, my_rows, :], recv.at[slot]
        ).start()

    def arrived(slot, dst):
        pltpu.make_async_copy(dst, dst, recv.at[slot]).wait()

    spread(0, k_in, kb, 0)

    local[2].wait()

    def gates(step, carry):
        for inner in range(4):
            at = aligned((step * 4 + inner) * DK, DK)
            for chain in range(2):
                scale[chain, :, at] = gain_in[0:1, at] * jax.nn.sigmoid(
                    gateb[chain, :, at].astype(F32)
                )
        return carry

    lax.fori_loop(0, H // 4, gates, 0)

    half = lb.at[:, aligned(core * (SPAN // 2), SPAN // 2), :]
    arrived(LAT, half)
    pass_on = pltpu.make_async_remote_copy(
        half, half, send.at[PASS], recv.at[PASS],
        device_id={"seq": seq + 1 - 2 * core}, device_id_type=MESH,
    )
    pass_on.start()
    spread(1, k_in, kb, 1)
    spread(2, v_in, vb, 0)
    spread(3, v_in, vb, 1)
    spread(4, q_in, qb, 0)
    spread(5, q_in, qb, 1)

    eye = ri == ci
    strict = ri > ci
    lower = ri >= ci
    tri = lower.astype(BF16)
    tri2 = jnp.concatenate([tri, tri], axis=1)
    upper = (ri <= ci).astype(BF16)
    lane = lax.broadcasted_iota(jnp.int32, (8, C), 1)
    local[0].wait()
    local[1].wait()
    arrived(AUX, auxb)
    pass_on.wait()

    rate = -jnp.exp(jnp.full((1, DK), rate_in[me], F32))

    def decays(step, carry):
        for inner in range(2):
            j = step * 2 + inner
            at = aligned(j * C, C)
            one = auxb[2 * j].astype(F32)
            two = auxb[2 * j + 1].astype(F32)
            mine = stack(
                jnp.where(lane < TOK, one, pltpu.roll(two, TOK, 1)),
                jnp.where(lane < TOK, pltpu.roll(one, TOK, 1), two),
            )
            counts = dot(mine.astype(BF16), upper)
            tall = stack(jax.nn.sigmoid(mine), counts, mine, jnp.zeros((C - 48, C), F32)).T
            cols[j] = tall
            rows[j] = counts
            for chain in range(2):
                kind = tall[:, 34 + 8 * chain:35 + 8 * chain]
                pre = dot(lb[chain, at, :], upb[...]).astype(BF16).astype(F32)
                bias = jnp.where(kind > 0.5, biasb[1:2, :], biasb[0:1, :])
                decay = rate * softplus(pre + bias)
                dh, dl = halves(decay)
                total[chain, at, :] = dot(tri2, stack(dh, dl))
        return carry

    lax.fori_loop(0, BLOCKS // 2, decays, 0)

    near = (ri // 16) == (ci // 16)

    def key_stage(chain):
        def body(step, carry):
            todo = []
            for inner in range(4):
                j = step * 4 + inner
                at = aligned(j * C, C)
                beta = cols[j, :, 8 * chain:8 * chain + 1]
                count_col = cols[j, :, 17 + 8 * chain:18 + 8 * chain]
                count_row = rows[j, 8 * chain + 1:8 * chain + 2, :]
                count_last = count_row[:, C - 1:C]
                sums = total[chain, at, :]
                last = sums[C - 1:C, :]
                growth = jnp.exp(sums)
                grow[chain, at, :] = growth
                key = unit(kb[chain, at, :])
                key_grow = key * growth
                alive = (count_col < 0.5).astype(F32)
                keyg[chain, at, :] = key_grow * (alive * beta)
                shrunk = halves(key * jnp.exp(-sums))
                shrink[chain, at, :] = jnp.concatenate(shrunk, axis=1)
                mask = (count_col == count_last).astype(F32)
                moved_t = halves((key * jnp.exp(last - sums) * mask).T)
                tail[chain, at, :] = jnp.concatenate(moved_t, axis=1)
                gram = lax.dot_general(
                    left_of(halves(key_grow)),
                    jnp.concatenate([shrunk[0], shrunk[0], shrunk[1]], axis=1),
                    (((1,), (1,)), ((), ())), preferred_element_type=F32,
                )
                low = jnp.where(strict & (count_col == count_row), gram, 0.0) * beta
                d = jnp.where(near, low, 0.0)
                todo.append(dict(at=at, low=low, d=d, ds=halves(d)))
            for t in todo:
                t["d2"] = fine(t["ds"], t["ds"])
                t["d2s"] = halves(t["d2"])
            for t in todo:
                both = dot(stack(left_of(t["ds"]), left_of(t["d2s"])), right_of(t["d2s"]))
                t["x"] = t["d2"] - t["d"] - both[:C]
                t["d4"] = both[C:]
                t["xs"], t["d4s"] = halves(t["x"]), halves(t["d4"])
            for t in todo:
                both = dot(stack(left_of(t["xs"]), left_of(t["d4s"])), right_of(t["d4s"]))
                t["x"] = t["x"] + t["d4"] + both[:C]
                t["d8"] = both[C:]
                t["xs"], t["d8s"] = halves(t["x"]), halves(t["d8"])
            for t in todo:
                t["x"] = t["x"] + t["d8"] + fine(t["xs"], t["d8s"])
                t["xs"] = halves(t["x"])
            width = 16
            while width < C:
                part = ((ri // (2 * width)) == (ci // (2 * width))) & (
                    (ri // width) != (ci // width)
                )
                for t in todo:
                    off = jnp.where(part, t["low"], 0.0)
                    t["ys"] = off + fine(halves(off), t["xs"])
                for t in todo:
                    t["x"] = t["x"] - (t["ys"] + fine(t["xs"], halves(t["ys"])))
                    t["xs"] = halves(t["x"])
                width *= 2
            for t in todo:
                xb[chain, t["at"], :] = jnp.concatenate(t["xs"], axis=1)
            return carry

        lax.fori_loop(0, BLOCKS // 4, body, 0)

    def value_stage(chain):
        maps[chain, :, 0:DK] = eye.astype(F32)
        maps[chain, :, DK:] = jnp.zeros((DK, DK), F32)

        def body(step, carry):
            todo = []
            for inner in range(4):
                j = step * 4 + inner
                at = aligned(j * C, C)
                beta = cols[j, :, 8 * chain:8 * chain + 1]
                count_last = rows[j, 8 * chain + 1:8 * chain + 2, C - 1:C]
                rhs = jnp.concatenate(
                    [keyg[chain, at, :], vb[chain, at, :].astype(F32) * beta], axis=1
                )
                xs = xb[chain, at, :]
                wu = rhs + dot(jnp.concatenate([xs, xs[:, :C]], axis=1), right_of(halves(rhs)))
                pair = halves(wu)
                wb[chain, at, :] = jnp.concatenate([pair[0][:, :C], pair[1][:, :C]], axis=1)
                ub[chain, at, :] = wu[:, C:]
                ts = tail[chain, at, :]
                both = dot(jnp.concatenate([ts, ts[:, :C]], axis=1), right_of(pair))
                carry_row = jnp.exp(total[chain, at, :][C - 1:C, :]) * (count_last < 0.5).astype(F32)
                move = jnp.where(eye, carry_row, 0.0) - both[:, :C]
                todo.append(dict(at=at, move=halves(move), offset=both[:, C:]))
            held = maps[chain]
            for t in todo:
                pair = halves(held)
                mcb[chain, t["at"], :] = jnp.concatenate(
                    [pair[0][:, :C], pair[1][:, :C]], axis=1
                )
                ocb[chain, t["at"], :] = held[:, C:]
                both = fine(t["move"], pair)
                held = jnp.concatenate([both[:, :C], both[:, C:] + t["offset"]], axis=1)
            maps[chain] = held
            return carry

        lax.fori_loop(0, BLOCKS // 4, body, 0)

    arrived(0, kb.at[0])
    key_stage(0)
    arrived(1, kb.at[1])
    key_stage(1)
    arrived(2, vb.at[0])
    value_stage(0)
    arrived(3, vb.at[1])
    value_stage(1)

    def send_to(src, dst, slot, to):
        return pltpu.make_async_remote_copy(
            src, dst, pre_send.at[slot], pre_recv.at[slot],
            device_id={"seq": 2 * to + core}, device_id_type=MESH,
        )

    moved[...] = maps[:, :, DK:]

    @pl.when(x == 0)
    def _():
        first[...] = jnp.zeros_like(first)
        send_to(moved, first, 0, 1).start()
        send_to(moved, first, 0, 1).wait_send()

    @pl.when(x == 2)
    def _():
        send_to(maps, second, 1, 3).start()

    @pl.when(x == 1)
    def _():
        send_to(moved, first, 0, 1).wait_recv()
        for chain in range(2):
            moved[chain] = maps[chain, :, DK:] + fine(
                halves(maps[chain, :, 0:DK]), halves(first[chain])
            )
        send_to(moved, first, 2, 3).start()
        send_to(moved, first, 0, 2).start()
        send_to(moved, first, 0, 2).wait_send()
        send_to(moved, first, 2, 3).wait_send()

    @pl.when(x == 2)
    def _():
        send_to(maps, second, 1, 3).wait_send()
        send_to(moved, first, 0, 2).wait_recv()

    @pl.when(x == 3)
    def _():
        send_to(maps, second, 1, 3).wait_recv()
        send_to(moved, first, 2, 3).wait_recv()
        for chain in range(2):
            first[chain] = second[chain, :, DK:] + fine(
                halves(second[chain, :, 0:DK]), halves(first[chain])
            )

    def state_stage(chain):
        incoming = right_of(halves(first[chain]))

        def body(step, carry):
            todo = []
            for inner in range(4):
                j = step * 4 + inner
                at = aligned(j * C, C)
                mc = mcb[chain, at, :]
                state = ocb[chain, at, :] + dot(
                    jnp.concatenate([mc, mc[:, :C]], axis=1), incoming
                )
                todo.append((j, at, halves(state)))
            for j, at, pair in todo:
                ws = wb[chain, at, :]
                fresh = ub[chain, at, :] - dot(
                    jnp.concatenate([ws, ws[:, :C]], axis=1), right_of(pair)
                )
                fh, fl = halves(fresh)
                right[chain, j] = stack(pair[0], fh, pair[1], fl)
            return carry

        lax.fori_loop(0, BLOCKS // 4, body, 0)

    state_stage(0)
    state_stage(1)

    def query_stage(chain):
        def body(step, carry):
            p = lax.rem(step + group // 2, BLOCKS // 2)
            for inner in range(2):
                j = 2 * p + inner
                at = aligned(j * C, C)
                count_col = cols[j, :, 17 + 8 * chain:18 + 8 * chain]
                count_row = rows[j, 8 * chain + 1:8 * chain + 2, :]
                query = unit(qb[chain, at, :]) * (DK ** -0.5) * grow[chain, at, :]
                sh = shrink[chain, at, :]
                gram = lax.dot_general(
                    left_of(halves(query)), jnp.concatenate([sh[:, :C], sh], axis=1),
                    (((1,), (1,)), ((), ())), preferred_element_type=F32,
                )
                mix = jnp.where(lower & (count_col == count_row), gram, 0.0)
                live = query * (count_col < 0.5).astype(F32)
                pair = halves(jnp.concatenate([live, mix], axis=1))
                hold = right[chain, j]
                out = dot(left_of(pair), stack(hold[:2 * C], hold))
                core_buf[chain, at, :] = out.astype(BF16)
            for inner in range(4):
                b = 4 * p + inner
                rows_b = aligned(b * TOK, TOK)
                src = core_buf.at[chain, rows_b, :]
                dst = back.at[chain, :, my_cols]

                @pl.when(b != blk)
                def _():
                    pltpu.make_async_remote_copy(
                        src, dst, back_send.at[chain], back_recv.at[chain],
                        device_id={"head": lax.rem(b, GROUPS), "seq": seq - core + b // GROUPS},
                        device_id_type=MESH,
                    ).start()

                @pl.when(b == blk)
                def _():
                    pltpu.make_async_copy(src, dst, back_recv.at[chain]).start()

            return carry

        lax.fori_loop(0, BLOCKS // 2, body, 0)

    arrived(4, qb.at[0])
    query_stage(0)
    arrived(5, qb.at[1])
    query_stage(1)

    for chain in range(2):
        pltpu.make_async_copy(back.at[chain], back.at[chain], back_recv.at[chain]).wait()

        def finish(step, carry, chain=chain):
            for inner in range(4):
                at = aligned((step * 4 + inner) * DK, DK)
                wide = back[chain, :, at].astype(F32)
                norm = lax.rsqrt(jnp.mean(wide * wide, axis=-1, keepdims=True) + NORM_EPS)
                out_ref[chain, :, at] = (wide * norm * scale[chain, :, at]).astype(BF16)
            return carry

        lax.fori_loop(0, H // 4, finish, 0)

    many = (OWNERS - 1) * DK
    for slot in range(6):
        sent = k_in.at[0, :, pl.ds(0, many)]
        pltpu.make_async_copy(sent, sent, send.at[slot]).wait()
    for chain in range(2):
        sent = back.at[0, :, pl.ds(0, many)]
        pltpu.make_async_copy(sent, sent, back_send.at[chain]).wait()
    lat_sent = lb.at[:, pl.ds(0, (GROUPS - 1) * TOK), :]
    pltpu.make_async_copy(lat_sent, lat_sent, send.at[LAT]).wait()
    aux_sent = aux_src.at[pl.ds(0, OWNERS - 1)]
    pltpu.make_async_copy(aux_sent, aux_sent, send.at[AUX]).wait()


def per_device(
    query_rows, key_rows, value_rows, beta_raw, gate_latent, gate_up, dt_bias, decay_log,
    boundary, modality, out_gate, norm_gain,
):
    span = lambda width, dtype: pltpu.VMEM((2, SPAN, width), dtype)
    return pl.pallas_call(
        kernel,
        out_shape=jax.ShapeDtypeStruct((2, TOK, H * DK), BF16),
        in_specs=[ANY, ANY, ANY, VM, VM, VM, ANY, ANY, ANY, SM, ANY, VM],
        out_specs=VM,
        scratch_shapes=[
            span(DK, BF16), span(DK, BF16), span(DK, BF16), span(DK, BF16),
            pltpu.VMEM((OWNERS, 8, C), BF16),
            pltpu.VMEM((OWNERS, 8, C), BF16),
            pltpu.VMEM((DK, DK), BF16),
            pltpu.VMEM((2, DK), F32),
            pltpu.VMEM((2, TOK, H * DK), BF16),
            pltpu.VMEM((2, TOK, H * DK), F32),
            span(DK, F32),
            span(DK, F32),
            span(2 * DK, BF16),
            span(DK, F32),
            span(2 * DK, BF16),
            span(2 * DK, BF16),
            span(2 * DK, BF16),
            span(DK, F32),
            span(2 * DK, BF16),
            span(DK, F32),
            pltpu.VMEM((2, BLOCKS, 4 * C, DK), BF16),
            pltpu.VMEM((BLOCKS, C, C), F32),
            pltpu.VMEM((BLOCKS, 16, C), F32),
            pltpu.VMEM((2, DK, 2 * DK), F32),
            pltpu.VMEM((2, DK, DK), F32),
            pltpu.VMEM((2, DK, 2 * DK), F32),
            pltpu.VMEM((2, DK, DK), F32),
            span(DK, BF16),
            pltpu.VMEM((2, TOK, H * DK), BF16),
            pltpu.SemaphoreType.DMA((9,)),
            pltpu.SemaphoreType.DMA((9,)),
            pltpu.SemaphoreType.DMA((3,)),
            pltpu.SemaphoreType.DMA((3,)),
            pltpu.SemaphoreType.DMA((2,)),
            pltpu.SemaphoreType.DMA((2,)),
            pltpu.SemaphoreType.DMA((3,)),
        ],
        compiler_params=pltpu.CompilerParams(
            collective_id=0, has_side_effects=True, vmem_limit_bytes=60 * 1024 * 1024
        ),
        name="delta_attention",
    )(
        query_rows, key_rows, value_rows, beta_raw.transpose(0, 2, 1), boundary, modality, gate_latent, gate_up, dt_bias, decay_log,
        out_gate, norm_gain.reshape(1, -1),
    )


def solution(mesh):
    rows = P(None, ("seq", "head"), None)
    flat = P(None, ("seq", "head"))
    return jax.shard_map(
        per_device,
        mesh=mesh,
        in_specs=(rows, rows, rows, rows, rows, P(), P(), P(), flat, flat, rows, P()),
        out_specs=rows,
        check_vma=False,
    )
```

time: 406 us -> 95.6 us (0.24)
  the two profiles are of different devices: /device:TPU:6 before, /device:TPU:7 now
where the time goes in v2:
time: 95.6 us; the launch traced here: 95.4 us
  Pallas kernels  93.1 us (97%)
  local copies, waits for them, and re-layouts  2.29 us (2%)
    pallas_call x1, Pallas kernels, per_device(): pl.pallas_call(kernel, out_shape=jax.ShapeDtypeStruct((2, TOK, H * DK), B...  93.1 us
    unnamed x1, local copies, waits for them, and re-layouts  2.29 us

profile of v2, /device:TPU:7, one launch (start us, length us, event | category | flops | bytes accessed | tf_op | source)
XLA Modules:
  0.0 95.4 jit_solution(10125692172817726001)
XLA Ops:
  0.0 93.1 %delta_attention.1 = bf16[2,64,4096]{2,1,0:T(8,128)(2,1)} custom-call(bf16[2,64,4096]{2,1,0:T(8,128)(2,1)} %q_in.1, bf16[2,64,4096]{2,1,0:T(8,128)(2,1)} %k_in.1, bf16[2,64,4096]{2,1,0:T(8,128)(2,1)} %v_in.1, bf16[2,32,64]{2,1,0:T(8,128)(2,1)} %bitcast.2, s32[2,64]{1,0:T(2,128)} %mark_in.1, s32[2,64]{1,0:T(2,128)} %kind_in.1, bf16[2,64,128]{2,1,0:T(8,128)(2,1)} %lat_in.1, ...), custom_call_target="tpu_custom_call" | custom-call | tf_op jit(solution)/shard_map/delta_attention/pallas_call | solution.py:494
  93.1 2.3 %copy.14 = bf16[2,64,4096]{2,1,0:T(8,128)(2,1)} copy(bf16[2,64,4096]{2,1,0:T(8,128)(2,1)} %delta_attention.1) | data formatting | bytes 2097152

commit v3 on v2

--- a/solution.py
+++ b/solution.py
@@ -21,6 +21,7 @@
 VM = pl.BlockSpec(memory_space=pltpu.VMEM)
 SM = pl.BlockSpec(memory_space=pltpu.SMEM)
 LAT, AUX, PASS = 6, 7, 8
+KEY_STEP = 8
 
 
 def halves(x):
@@ -68,7 +69,7 @@
     out_ref,
     kb, vb, qb, lb, auxb, aux_src, upb, biasb, gateb, scale,
     total, grow, shrink, keyg, tail, xb, wb, ub, mcb, ocb, right, cols, rows,
-    maps, first, second, moved, core_buf, back,
+    maps, first, gathered, leftb, core_buf, back,
     send, recv, pre_send, pre_recv, back_send, back_recv, here,
 ):
     group = lax.axis_index("head")
@@ -204,8 +205,8 @@
     rate = -jnp.exp(jnp.full((1, DK), rate_in[me], F32))
 
     def decays(step, carry):
-        for inner in range(2):
-            j = step * 2 + inner
+        for inner in range(4):
+            j = step * 4 + inner
             at = aligned(j * C, C)
             one = auxb[2 * j].astype(F32)
             two = auxb[2 * j + 1].astype(F32)
@@ -226,15 +227,15 @@
                 total[chain, at, :] = dot(tri2, stack(dh, dl))
         return carry
 
-    lax.fori_loop(0, BLOCKS // 2, decays, 0)
+    lax.fori_loop(0, BLOCKS // 4, decays, 0)
 
     near = (ri // 16) == (ci // 16)
 
     def key_stage(chain):
         def body(step, carry):
             todo = []
-            for inner in range(4):
-                j = step * 4 + inner
+            for inner in range(KEY_STEP):
+                j = step * KEY_STEP + inner
                 at = aligned(j * C, C)
                 beta = cols[j, :, 8 * chain:8 * chain + 1]
                 count_col = cols[j, :, 17 + 8 * chain:18 + 8 * chain]
@@ -254,46 +255,43 @@
                 moved_t = halves((key * jnp.exp(last - sums) * mask).T)
                 tail[chain, at, :] = jnp.concatenate(moved_t, axis=1)
                 gram = lax.dot_general(
-                    left_of(halves(key_grow)),
-                    jnp.concatenate([shrunk[0], shrunk[0], shrunk[1]], axis=1),
+                    key_grow.astype(BF16), shrunk[0],
                     (((1,), (1,)), ((), ())), preferred_element_type=F32,
                 )
                 low = jnp.where(strict & (count_col == count_row), gram, 0.0) * beta
                 d = jnp.where(near, low, 0.0)
-                todo.append(dict(at=at, low=low, d=d, ds=halves(d)))
+                todo.append(dict(at=at, low=low, d=d, db=d.astype(BF16)))
             for t in todo:
-                t["d2"] = fine(t["ds"], t["ds"])
-                t["d2s"] = halves(t["d2"])
+                t["d2"] = dot(t["db"], t["db"])
+                t["d2b"] = t["d2"].astype(BF16)
             for t in todo:
-                both = dot(stack(left_of(t["ds"]), left_of(t["d2s"])), right_of(t["d2s"]))
+                both = dot(stack(t["db"], t["d2b"]), t["d2b"])
                 t["x"] = t["d2"] - t["d"] - both[:C]
                 t["d4"] = both[C:]
-                t["xs"], t["d4s"] = halves(t["x"]), halves(t["d4"])
             for t in todo:
-                both = dot(stack(left_of(t["xs"]), left_of(t["d4s"])), right_of(t["d4s"]))
+                d4b = t["d4"].astype(BF16)
+                both = dot(stack(t["x"].astype(BF16), d4b), d4b)
                 t["x"] = t["x"] + t["d4"] + both[:C]
                 t["d8"] = both[C:]
-                t["xs"], t["d8s"] = halves(t["x"]), halves(t["d8"])
             for t in todo:
-                t["x"] = t["x"] + t["d8"] + fine(t["xs"], t["d8s"])
-                t["xs"] = halves(t["x"])
+                t["x"] = t["x"] + t["d8"] + dot(t["x"].astype(BF16), t["d8"].astype(BF16))
             width = 16
             while width < C:
                 part = ((ri // (2 * width)) == (ci // (2 * width))) & (
                     (ri // width) != (ci // width)
                 )
                 for t in todo:
-                    off = jnp.where(part, t["low"], 0.0)
-                    t["ys"] = off + fine(halves(off), t["xs"])
+                    t["off"] = jnp.where(part, t["low"], 0.0)
+                    t["xs"] = t["x"].astype(BF16)
+                    t["y"] = t["off"] + dot(t["off"].astype(BF16), t["xs"])
                 for t in todo:
-                    t["x"] = t["x"] - (t["ys"] + fine(t["xs"], halves(t["ys"])))
-                    t["xs"] = halves(t["x"])
+                    t["x"] = t["x"] - (t["y"] + dot(t["xs"], t["y"].astype(BF16)))
                 width *= 2
             for t in todo:
-                xb[chain, t["at"], :] = jnp.concatenate(t["xs"], axis=1)
+                xb[chain, t["at"], :] = t["x"].astype(BF16)
             return carry
 
-        lax.fori_loop(0, BLOCKS // 4, body, 0)
+        lax.fori_loop(0, BLOCKS // KEY_STEP, body, 0)
 
     def value_stage(chain):
         maps[chain, :, 0:DK] = eye.astype(F32)
@@ -309,8 +307,7 @@
                 rhs = jnp.concatenate(
                     [keyg[chain, at, :], vb[chain, at, :].astype(F32) * beta], axis=1
                 )
-                xs = xb[chain, at, :]
-                wu = rhs + dot(jnp.concatenate([xs, xs[:, :C]], axis=1), right_of(halves(rhs)))
+                wu = rhs + dot(xb[chain, at, :], rhs.astype(BF16))
                 pair = halves(wu)
                 wb[chain, at, :] = jnp.concatenate([pair[0][:, :C], pair[1][:, :C]], axis=1)
                 ub[chain, at, :] = wu[:, C:]
@@ -318,20 +315,53 @@
                 both = dot(jnp.concatenate([ts, ts[:, :C]], axis=1), right_of(pair))
                 carry_row = jnp.exp(total[chain, at, :][C - 1:C, :]) * (count_last < 0.5).astype(F32)
                 move = jnp.where(eye, carry_row, 0.0) - both[:, :C]
-                todo.append(dict(at=at, move=halves(move), offset=both[:, C:]))
-            held = maps[chain]
-            for t in todo:
-                pair = halves(held)
-                mcb[chain, t["at"], :] = jnp.concatenate(
-                    [pair[0][:, :C], pair[1][:, :C]], axis=1
-                )
-                ocb[chain, t["at"], :] = held[:, C:]
-                both = fine(t["move"], pair)
-                held = jnp.concatenate([both[:, :C], both[:, C:] + t["offset"]], axis=1)
-            maps[chain] = held
+                todo.append((at, move, both[:, C:]))
+
+            def chained(move, offset, pair):
+                both = fine(move, pair)
+                return jnp.concatenate([both[:, :C], both[:, C:] + offset], axis=1)
+
+            def keep(at, pair, offset):
+                mcb[chain, at, :] = jnp.concatenate([pair[0][:, :C], pair[1][:, :C]], axis=1)
+                ocb[chain, at, :] = offset
+
+            one = halves(jnp.concatenate(todo[0][1:], axis=1))
+            two = chained(halves(todo[1][1]), todo[1][2], one)
+            rest = chained(
+                halves(todo[3][1]), todo[3][2], halves(jnp.concatenate(todo[2][1:], axis=1))
+            )
+            two_s = halves(two)
+            three = chained(halves(todo[2][1]), todo[2][2], two_s)
+            four = chained(halves(rest[:, :C]), rest[:, C:], two_s)
+            four_m = halves(four[:, :C])
+            keep(todo[1][0], one, todo[0][2])
+            keep(todo[2][0], two_s, two[:, C:])
+            keep(todo[3][0], halves(three[:, :C]), three[:, C:])
+            keep(todo[0][0], four_m, four[:, C:])
+            maps[chain] = chained(four_m, four[:, C:], halves(maps[chain]))
             return carry
 
         lax.fori_loop(0, BLOCKS // 4, body, 0)
+
+    def map_copy(chain, src_x, to):
+        cut = pl.ds(DK, DK) if src_x == 0 else pl.ds(0, 2 * DK)
+        return pltpu.make_async_remote_copy(
+            maps.at[chain, :, cut], gathered.at[src_x, chain, :, cut],
+            pre_send.at[chain, to - 1], pre_recv.at[chain, src_x],
+            device_id={"seq": 2 * to + core}, device_id_type=MESH,
+        )
+
+    def map_sends(chain, wait):
+        for src_x in range(3):
+
+            @pl.when(x == src_x)
+            def _():
+                for to in range(src_x + 1, 4):
+                    copy = map_copy(chain, src_x, to)
+                    if wait:
+                        copy.wait_send()
+                    else:
+                        copy.start()
 
     arrived(0, kb.at[0])
     key_stage(0)
@@ -339,104 +369,95 @@
     key_stage(1)
     arrived(2, vb.at[0])
     value_stage(0)
+    map_sends(0, False)
     arrived(3, vb.at[1])
     value_stage(1)
-
-    def send_to(src, dst, slot, to):
-        return pltpu.make_async_remote_copy(
-            src, dst, pre_send.at[slot], pre_recv.at[slot],
-            device_id={"seq": 2 * to + core}, device_id_type=MESH,
+    map_sends(1, False)
+
+    def query_parts(chain, j):
+        at = aligned(j * C, C)
+        count_col = cols[j, :, 17 + 8 * chain:18 + 8 * chain]
+        count_row = rows[j, 8 * chain + 1:8 * chain + 2, :]
+        query = unit(qb[chain, at, :]) * (DK ** -0.5) * grow[chain, at, :]
+        sh = shrink[chain, at, :]
+        gram = lax.dot_general(
+            left_of(halves(query)), jnp.concatenate([sh[:, :C], sh], axis=1),
+            (((1,), (1,)), ((), ())), preferred_element_type=F32,
         )
-
-    moved[...] = maps[:, :, DK:]
+        mix = jnp.where(lower & (count_col == count_row), gram, 0.0)
+        live = query * (count_col < 0.5).astype(F32)
+        return halves(jnp.concatenate([live, mix], axis=1))
+
+    def query_stage(step, carry):
+        for inner in range(4):
+            j = step * 4 + inner
+            leftb[aligned(j * C, C), :] = jnp.concatenate(query_parts(0, j), axis=1)
+        return carry
+
+    arrived(4, qb.at[0])
+    lax.fori_loop(0, BLOCKS // 4, query_stage, 0)
 
     @pl.when(x == 0)
     def _():
         first[...] = jnp.zeros_like(first)
-        send_to(moved, first, 0, 1).start()
-        send_to(moved, first, 0, 1).wait_send()
-
-    @pl.when(x == 2)
-    def _():
-        send_to(maps, second, 1, 3).start()
-
-    @pl.when(x == 1)
-    def _():
-        send_to(moved, first, 0, 1).wait_recv()
+
+    for src_x in range(3):
+
+        @pl.when(x > src_x)
+        def _():
+            for chain in range(2):
+                map_copy(chain, src_x, src_x + 1).wait_recv()
+                if src_x == 0:
+                    first[chain] = gathered[0, chain, :, DK:]
+                else:
+                    first[chain] = gathered[src_x, chain, :, DK:] + fine(
+                        halves(gathered[src_x, chain, :, 0:DK]), halves(first[chain])
+                    )
+
+    def state_stage(step, carry):
         for chain in range(2):
-            moved[chain] = maps[chain, :, DK:] + fine(
-                halves(maps[chain, :, 0:DK]), halves(first[chain])
-            )
-        send_to(moved, first, 2, 3).start()
-        send_to(moved, first, 0, 2).start()
-        send_to(moved, first, 0, 2).wait_send()
-        send_to(moved, first, 2, 3).wait_send()
-
-    @pl.when(x == 2)
-    def _():
-        send_to(maps, second, 1, 3).wait_send()
-        send_to(moved, first, 0, 2).wait_recv()
-
-    @pl.when(x == 3)
-    def _():
-        send_to(maps, second, 1, 3).wait_recv()
-        send_to(moved, first, 2, 3).wait_recv()
-        for chain in range(2):
-            first[chain] = second[chain, :, DK:] + fine(
-                halves(second[chain, :, 0:DK]), halves(first[chain])
-            )
-
-    def state_stage(chain):
-        incoming = right_of(halves(first[chain]))
-
-        def body(step, carry):
-            todo = []
+            now = first[chain]
+            now_s = halves(now)
+            incoming = right_of(now_s)
+
+            def moved(at):
+                mc = mcb[chain, at, :]
+                return ocb[chain, at, :] + dot(
+                    jnp.concatenate([mc, mc[:, :C]], axis=1), incoming
+                )
+
             for inner in range(4):
                 j = step * 4 + inner
                 at = aligned(j * C, C)
-                mc = mcb[chain, at, :]
-                state = ocb[chain, at, :] + dot(
-                    jnp.concatenate([mc, mc[:, :C]], axis=1), incoming
-                )
-                todo.append((j, at, halves(state)))
-            for j, at, pair in todo:
+                pair = now_s if inner == 0 else halves(moved(at))
                 ws = wb[chain, at, :]
                 fresh = ub[chain, at, :] - dot(
                     jnp.concatenate([ws, ws[:, :C]], axis=1), right_of(pair)
                 )
                 fh, fl = halves(fresh)
                 right[chain, j] = stack(pair[0], fh, pair[1], fl)
-            return carry
-
-        lax.fori_loop(0, BLOCKS // 4, body, 0)
-
-    state_stage(0)
-    state_stage(1)
-
-    def query_stage(chain):
+            first[chain] = moved(aligned(step * 4 * C, C))
+        return carry
+
+    lax.fori_loop(0, BLOCKS // 4, state_stage, 0)
+
+    def output_stage(chain):
         def body(step, carry):
-            p = lax.rem(step + group // 2, BLOCKS // 2)
-            for inner in range(2):
-                j = 2 * p + inner
+            p = lax.rem(step + group // 4, BLOCKS // 4)
+            for inner in range(4):
+                j = 4 * p + inner
                 at = aligned(j * C, C)
-                count_col = cols[j, :, 17 + 8 * chain:18 + 8 * chain]
-                count_row = rows[j, 8 * chain + 1:8 * chain + 2, :]
-                query = unit(qb[chain, at, :]) * (DK ** -0.5) * grow[chain, at, :]
-                sh = shrink[chain, at, :]
-                gram = lax.dot_general(
-                    left_of(halves(query)), jnp.concatenate([sh[:, :C], sh], axis=1),
-                    (((1,), (1,)), ((), ())), preferred_element_type=F32,
-                )
-                mix = jnp.where(lower & (count_col == count_row), gram, 0.0)
-                live = query * (count_col < 0.5).astype(F32)
-                pair = halves(jnp.concatenate([live, mix], axis=1))
+                if chain == 0:
+                    ls = leftb[at, :]
+                    left = jnp.concatenate([ls, ls[:, :2 * C]], axis=1)
+                else:
+                    left = left_of(query_parts(chain, j))
                 hold = right[chain, j]
-                out = dot(left_of(pair), stack(hold[:2 * C], hold))
+                out = dot(left, stack(hold[:2 * C], hold))
                 core_buf[chain, at, :] = out.astype(BF16)
-            for inner in range(4):
-                b = 4 * p + inner
-                rows_b = aligned(b * TOK, TOK)
-                src = core_buf.at[chain, rows_b, :]
+            for inner in range(8):
+                b = 8 * p + inner
+                src = core_buf.at[chain, aligned(b * TOK, TOK), :]
                 dst = back.at[chain, :, my_cols]
 
                 @pl.when(b != blk)
@@ -453,25 +474,27 @@
 
             return carry
 
-        lax.fori_loop(0, BLOCKS // 2, body, 0)
-
-    arrived(4, qb.at[0])
-    query_stage(0)
+        lax.fori_loop(0, BLOCKS // 4, body, 0)
+
+    output_stage(0)
     arrived(5, qb.at[1])
-    query_stage(1)
+    output_stage(1)
 
     for chain in range(2):
         pltpu.make_async_copy(back.at[chain], back.at[chain], back_recv.at[chain]).wait()
 
         def finish(step, carry, chain=chain):
-            for inner in range(4):
-                at = aligned((step * 4 + inner) * DK, DK)
+            for inner in range(8):
+                at = aligned((step * 8 + inner) * DK, DK)
                 wide = back[chain, :, at].astype(F32)
                 norm = lax.rsqrt(jnp.mean(wide * wide, axis=-1, keepdims=True) + NORM_EPS)
                 out_ref[chain, :, at] = (wide * norm * scale[chain, :, at]).astype(BF16)
             return carry
 
-        lax.fori_loop(0, H // 4, finish, 0)
+        lax.fori_loop(0, H // 8, finish, 0)
+
+    map_sends(0, True)
+    map_sends(1, True)
 
     many = (OWNERS - 1) * DK
     for slot in range(6):
@@ -509,7 +532,7 @@
             span(2 * DK, BF16),
             span(DK, F32),
             span(2 * DK, BF16),
-            span(2 * DK, BF16),
+            span(DK, BF16),
             span(2 * DK, BF16),
             span(DK, F32),
             span(2 * DK, BF16),
@@ -519,14 +542,14 @@
             pltpu.VMEM((BLOCKS, 16, C), F32),
             pltpu.VMEM((2, DK, 2 * DK), F32),
             pltpu.VMEM((2, DK, DK), F32),
-            pltpu.VMEM((2, DK, 2 * DK), F32),
-            pltpu.VMEM((2, DK, DK), F32),
+            pltpu.VMEM((3, 2, DK, 2 * DK), F32),
+            pltpu.VMEM((SPAN, 4 * C), BF16),
             span(DK, BF16),
             pltpu.VMEM((2, TOK, H * DK), BF16),
             pltpu.SemaphoreType.DMA((9,)),
             pltpu.SemaphoreType.DMA((9,)),
-            pltpu.SemaphoreType.DMA((3,)),
-            pltpu.SemaphoreType.DMA((3,)),
+            pltpu.SemaphoreType.DMA((2, 3)),
+            pltpu.SemaphoreType.DMA((2, 3)),
             pltpu.SemaphoreType.DMA((2,)),
             pltpu.SemaphoreType.DMA((2,)),
             pltpu.SemaphoreType.DMA((3,)),

time: 95.6 us -> 83.9 us (0.88)
  the two profiles are of different devices: /device:TPU:7 before, /device:TPU:6 now
where the time goes in v3:
time: 83.9 us; the launch traced here: 83.7 us
  Pallas kernels  81.4 us (97%)
  local copies, waits for them, and re-layouts  2.29 us (3%)
    pallas_call x1, Pallas kernels, per_device(): pl.pallas_call(kernel, out_shape=jax.ShapeDtypeStruct((2, TOK, H * DK), B...  81.4 us
    unnamed x1, local copies, waits for them, and re-layouts  2.29 us

profile of v3, /device:TPU:6, one launch (start us, length us, event | category | flops | bytes accessed | tf_op | source)
XLA Modules:
  0.0 83.7 jit_solution(7218094738377497405)
XLA Ops:
  0.0 81.4 %delta_attention.1 = bf16[2,64,4096]{2,1,0:T(8,128)(2,1)} custom-call(bf16[2,64,4096]{2,1,0:T(8,128)(2,1)} %q_in.1, bf16[2,64,4096]{2,1,0:T(8,128)(2,1)} %k_in.1, bf16[2,64,4096]{2,1,0:T(8,128)(2,1)} %v_in.1, bf16[2,32,64]{2,1,0:T(8,128)(2,1)} %bitcast.2, s32[2,64]{1,0:T(2,128)} %mark_in.1, s32[2,64]{1,0:T(2,128)} %kind_in.1, bf16[2,64,128]{2,1,0:T(8,128)(2,1)} %lat_in.1, ...), custom_call_target="tpu_custom_call" | custom-call | tf_op jit(solution)/shard_map/delta_attention/pallas_call | solution.py:517
  81.4 2.3 %copy.14 = bf16[2,64,4096]{2,1,0:T(8,128)(2,1)} copy(bf16[2,64,4096]{2,1,0:T(8,128)(2,1)} %delta_attention.1) | data formatting | bytes 2097152

commit v4 on v3

--- a/solution.py
+++ b/solution.py
@@ -1,3 +1,5 @@
+import functools
+
 import jax
 import jax.numpy as jnp
 from jax import lax
@@ -69,7 +71,7 @@
     out_ref,
     kb, vb, qb, lb, auxb, aux_src, upb, biasb, gateb, scale,
     total, grow, shrink, keyg, tail, xb, wb, ub, mcb, ocb, right, cols, rows,
-    maps, first, gathered, leftb, core_buf, back,
+    maps, first, gathered, states, leftb, core_buf, back,
     send, recv, pre_send, pre_recv, back_send, back_recv, here,
 ):
     group = lax.axis_index("head")
@@ -127,7 +129,7 @@
     def lat_send(step, carry):
         pltpu.make_async_remote_copy(
             lat_in, lb.at[:, my_rows, :], send.at[LAT], recv.at[LAT],
-            device_id={"head": lax.rem(group + step, GROUPS), "seq": seq}, device_id_type=MESH,
+            device_id={"head": lax.rem(group + 5 * step, GROUPS), "seq": seq}, device_id_type=MESH,
         ).start()
         return carry
 
@@ -147,7 +149,7 @@
 
     def spread(slot, src, dst, chain):
         def one(step, carry):
-            other = lax.rem(me + step, OWNERS)
+            other = lax.rem(me + 5 * step, OWNERS)
             pltpu.make_async_remote_copy(
                 src.at[chain, :, aligned(other * DK, DK)], dst.at[chain, my_rows, :],
                 send.at[slot], recv.at[slot], device_id=owner_id(other), device_id_type=MESH,
@@ -200,13 +202,12 @@
     local[0].wait()
     local[1].wait()
     arrived(AUX, auxb)
-    pass_on.wait()
 
     rate = -jnp.exp(jnp.full((1, DK), rate_in[me], F32))
 
-    def decays(step, carry):
+    def decays(step, start):
         for inner in range(4):
-            j = step * 4 + inner
+            j = lax.rem(start + step * 4 + inner, BLOCKS)
             at = aligned(j * C, C)
             one = auxb[2 * j].astype(F32)
             two = auxb[2 * j + 1].astype(F32)
@@ -225,11 +226,19 @@
                 decay = rate * softplus(pre + bias)
                 dh, dl = halves(decay)
                 total[chain, at, :] = dot(tri2, stack(dh, dl))
-        return carry
-
-    lax.fori_loop(0, BLOCKS // 4, decays, 0)
-
-    near = (ri // 16) == (ci // 16)
+        return start
+
+    lax.fori_loop(0, BLOCKS // 8, decays, core * (BLOCKS // 2))
+    pass_on.wait()
+    lax.fori_loop(0, BLOCKS // 8, decays, (1 - core) * (BLOCKS // 2))
+
+    near = ((ri // 16) == (ci // 16)).astype(BF16)
+    eye_wide = eye.astype(F32)
+    eye_low = eye.astype(BF16)
+    parts = []
+    for width in (16, 32, 64):
+        same_pair = (ri // (2 * width)) == (ci // (2 * width))
+        parts.append((same_pair & ((ri // width) != (ci // width))).astype(BF16))
 
     def key_stage(chain):
         def body(step, carry):
@@ -259,36 +268,29 @@
                     (((1,), (1,)), ((), ())), preferred_element_type=F32,
                 )
                 low = jnp.where(strict & (count_col == count_row), gram, 0.0) * beta
-                d = jnp.where(near, low, 0.0)
-                todo.append(dict(at=at, low=low, d=d, db=d.astype(BF16)))
+                low = low.astype(BF16)
+                todo.append(dict(at=at, low=low, d=low * near))
             for t in todo:
-                t["d2"] = dot(t["db"], t["db"])
-                t["d2b"] = t["d2"].astype(BF16)
+                t["d2"] = dot(t["d"], t["d"]).astype(BF16)
             for t in todo:
-                both = dot(stack(t["db"], t["d2b"]), t["d2b"])
-                t["x"] = t["d2"] - t["d"] - both[:C]
-                t["d4"] = both[C:]
+                start = eye_low - t["d"]
+                both = dot(stack(start, t["d2"]), t["d2"])
+                t["t"] = start.astype(F32) + both[:C]
+                t["d4"] = both[C:].astype(BF16)
             for t in todo:
-                d4b = t["d4"].astype(BF16)
-                both = dot(stack(t["x"].astype(BF16), d4b), d4b)
-                t["x"] = t["x"] + t["d4"] + both[:C]
-                t["d8"] = both[C:]
+                both = dot(stack(t["t"].astype(BF16), t["d4"]), t["d4"])
+                t["t"] = t["t"] + both[:C]
+                t["d8"] = both[C:].astype(BF16)
             for t in todo:
-                t["x"] = t["x"] + t["d8"] + dot(t["x"].astype(BF16), t["d8"].astype(BF16))
-            width = 16
-            while width < C:
-                part = ((ri // (2 * width)) == (ci // (2 * width))) & (
-                    (ri // width) != (ci // width)
-                )
+                t["t"] = t["t"] + dot(t["t"].astype(BF16), t["d8"])
+            for part in parts:
                 for t in todo:
-                    t["off"] = jnp.where(part, t["low"], 0.0)
-                    t["xs"] = t["x"].astype(BF16)
-                    t["y"] = t["off"] + dot(t["off"].astype(BF16), t["xs"])
+                    t["tb"] = t["t"].astype(BF16)
+                    t["y"] = dot(t["low"] * part, t["tb"]).astype(BF16)
                 for t in todo:
-                    t["x"] = t["x"] - (t["y"] + dot(t["xs"], t["y"].astype(BF16)))
-                width *= 2
+                    t["t"] = t["t"] - dot(t["tb"], t["y"])
             for t in todo:
-                xb[chain, t["at"], :] = t["x"].astype(BF16)
+                xb[chain, t["at"], :] = (t["t"] - eye_wide).astype(BF16)
             return carry
 
         lax.fori_loop(0, BLOCKS // KEY_STEP, body, 0)
@@ -299,8 +301,8 @@
 
         def body(step, carry):
             todo = []
-            for inner in range(4):
-                j = step * 4 + inner
+            for inner in range(8):
+                j = step * 8 + inner
                 at = aligned(j * C, C)
                 beta = cols[j, :, 8 * chain:8 * chain + 1]
                 count_last = rows[j, 8 * chain + 1:8 * chain + 2, C - 1:C]
@@ -325,23 +327,29 @@
                 mcb[chain, at, :] = jnp.concatenate([pair[0][:, :C], pair[1][:, :C]], axis=1)
                 ocb[chain, at, :] = offset
 
-            one = halves(jnp.concatenate(todo[0][1:], axis=1))
-            two = chained(halves(todo[1][1]), todo[1][2], one)
-            rest = chained(
-                halves(todo[3][1]), todo[3][2], halves(jnp.concatenate(todo[2][1:], axis=1))
-            )
-            two_s = halves(two)
-            three = chained(halves(todo[2][1]), todo[2][2], two_s)
-            four = chained(halves(rest[:, :C]), rest[:, C:], two_s)
-            four_m = halves(four[:, :C])
-            keep(todo[1][0], one, todo[0][2])
-            keep(todo[2][0], two_s, two[:, C:])
-            keep(todo[3][0], halves(three[:, :C]), three[:, C:])
-            keep(todo[0][0], four_m, four[:, C:])
-            maps[chain] = chained(four_m, four[:, C:], halves(maps[chain]))
+            past = []
+            for four_of in (todo[:4], todo[4:]):
+                one = halves(jnp.concatenate(four_of[0][1:], axis=1))
+                two = chained(halves(four_of[1][1]), four_of[1][2], one)
+                rest = chained(
+                    halves(four_of[3][1]), four_of[3][2], halves(jnp.concatenate(four_of[2][1:], axis=1))
+                )
+                two_s = halves(two)
+                three = chained(halves(four_of[2][1]), four_of[2][2], two_s)
+                four = chained(halves(rest[:, :C]), rest[:, C:], two_s)
+                four_m = halves(four[:, :C])
+                keep(four_of[1][0], one, four_of[0][2])
+                keep(four_of[2][0], two_s, two[:, C:])
+                keep(four_of[3][0], halves(three[:, :C]), three[:, C:])
+                keep(four_of[0][0], four_m, four[:, C:])
+                past.append((four_m, four[:, C:]))
+            held = maps[chain]
+            for move, offset in past:
+                held = chained(move, offset, halves(held))
+            maps[chain] = held
             return carry
 
-        lax.fori_loop(0, BLOCKS // 4, body, 0)
+        lax.fori_loop(0, BLOCKS // 8, body, 0)
 
     def map_copy(chain, src_x, to):
         cut = pl.ds(DK, DK) if src_x == 0 else pl.ds(0, 2 * DK)
@@ -388,14 +396,14 @@
         live = query * (count_col < 0.5).astype(F32)
         return halves(jnp.concatenate([live, mix], axis=1))
 
-    def query_stage(step, carry):
+    def query_stage(step, carry, chain):
         for inner in range(4):
             j = step * 4 + inner
-            leftb[aligned(j * C, C), :] = jnp.concatenate(query_parts(0, j), axis=1)
+            leftb[aligned(j * C, C), :] = jnp.concatenate(query_parts(chain, j), axis=1)
         return carry
 
     arrived(4, qb.at[0])
-    lax.fori_loop(0, BLOCKS // 4, query_stage, 0)
+    lax.fori_loop(0, BLOCKS // 4, functools.partial(query_stage, chain=0), 0)
 
     @pl.when(x == 0)
     def _():
@@ -414,70 +422,76 @@
                         halves(gathered[src_x, chain, :, 0:DK]), halves(first[chain])
                     )
 
-    def state_stage(step, carry):
+    def moved(chain, at, incoming):
+        mc = mcb[chain, at, :]
+        return ocb[chain, at, :] + dot(jnp.concatenate([mc, mc[:, :C]], axis=1), incoming)
+
+    now = [first[0], first[1]]
+    for four in range(BLOCKS // 4):
         for chain in range(2):
-            now = first[chain]
-            now_s = halves(now)
-            incoming = right_of(now_s)
-
-            def moved(at):
-                mc = mcb[chain, at, :]
-                return ocb[chain, at, :] + dot(
-                    jnp.concatenate([mc, mc[:, :C]], axis=1), incoming
-                )
-
-            for inner in range(4):
-                j = step * 4 + inner
+            incoming = right_of(halves(now[chain]))
+            states[chain, four] = incoming
+            if four < BLOCKS // 4 - 1:
+                now[chain] = moved(chain, pl.ds(four * 4 * C, C), incoming)
+
+    def state_stage(chain):
+        def body(step, carry):
+            todo = []
+            for inner in range(8):
+                j = step * 8 + inner
                 at = aligned(j * C, C)
-                pair = now_s if inner == 0 else halves(moved(at))
+                incoming = states[chain, step * 2 + inner // 4]
+                if inner % 4 == 0:
+                    todo.append((j, at, incoming))
+                else:
+                    todo.append((j, at, right_of(halves(moved(chain, at, incoming)))))
+            for j, at, incoming in todo:
                 ws = wb[chain, at, :]
-                fresh = ub[chain, at, :] - dot(
-                    jnp.concatenate([ws, ws[:, :C]], axis=1), right_of(pair)
-                )
+                fresh = ub[chain, at, :] - dot(jnp.concatenate([ws, ws[:, :C]], axis=1), incoming)
                 fh, fl = halves(fresh)
-                right[chain, j] = stack(pair[0], fh, pair[1], fl)
-            first[chain] = moved(aligned(step * 4 * C, C))
-        return carry
-
-    lax.fori_loop(0, BLOCKS // 4, state_stage, 0)
+                right[chain, j] = stack(incoming[C:2 * C], fh, incoming[2 * C:], fl)
+            return carry
+
+        lax.fori_loop(0, BLOCKS // 8, body, 0)
 
     def output_stage(chain):
-        def body(step, carry):
-            p = lax.rem(step + group // 4, BLOCKS // 4)
+        def body(step, own):
+            p = lax.rem(step + blk // 8, BLOCKS // 4)
             for inner in range(4):
                 j = 4 * p + inner
                 at = aligned(j * C, C)
-                if chain == 0:
-                    ls = leftb[at, :]
-                    left = jnp.concatenate([ls, ls[:, :2 * C]], axis=1)
-                else:
-                    left = left_of(query_parts(chain, j))
+                ls = leftb[at, :]
                 hold = right[chain, j]
-                out = dot(left, stack(hold[:2 * C], hold))
+                out = dot(
+                    jnp.concatenate([ls, ls[:, :2 * C]], axis=1), stack(hold[:2 * C], hold)
+                )
                 core_buf[chain, at, :] = out.astype(BF16)
             for inner in range(8):
-                b = 8 * p + inner
+                b = 8 * p + lax.rem(blk + inner, 8)
                 src = core_buf.at[chain, aligned(b * TOK, TOK), :]
                 dst = back.at[chain, :, my_cols]
-
-                @pl.when(b != blk)
-                def _():
+                if own and inner == 0:
+                    pltpu.make_async_copy(src, dst, back_recv.at[chain]).start()
+                else:
                     pltpu.make_async_remote_copy(
                         src, dst, back_send.at[chain], back_recv.at[chain],
                         device_id={"head": lax.rem(b, GROUPS), "seq": seq - core + b // GROUPS},
                         device_id_type=MESH,
                     ).start()
 
-                @pl.when(b == blk)
-                def _():
-                    pltpu.make_async_copy(src, dst, back_recv.at[chain]).start()
-
+        body(0, True)
+
+        def others(step, carry):
+            body(step, False)
             return carry
 
-        lax.fori_loop(0, BLOCKS // 4, body, 0)
-
+        lax.fori_loop(1, BLOCKS // 4, others, 0)
+
+    state_stage(0)
     output_stage(0)
+    state_stage(1)
     arrived(5, qb.at[1])
+    lax.fori_loop(0, BLOCKS // 4, functools.partial(query_stage, chain=1), 0)
     output_stage(1)
 
     for chain in range(2):
@@ -543,6 +557,7 @@
             pltpu.VMEM((2, DK, 2 * DK), F32),
             pltpu.VMEM((2, DK, DK), F32),
             pltpu.VMEM((3, 2, DK, 2 * DK), F32),
+            pltpu.VMEM((2, BLOCKS // 4, 3 * C, DK), BF16),
             pltpu.VMEM((SPAN, 4 * C), BF16),
             span(DK, BF16),
             pltpu.VMEM((2, TOK, H * DK), BF16),

time: 83.9 us -> 72 us (0.86); the launches traced: 83.7 us -> 70.9 us
  Pallas kernels: 81.4 us -> 68.6 us
    pallas_call x1, Pallas kernels: 81.4 us -> 68.6 us  [per_device(): pl.pallas_call(kernel, out_shape=jax.ShapeDtypeStruct((2, TOK, H * DK), B...]
where the time goes in v4:
time: 72 us; the launch traced here: 70.9 us
  Pallas kernels  68.6 us (95%)
  local copies, waits for them, and re-layouts  2.29 us (3%)
    pallas_call x1, Pallas kernels, per_device(): pl.pallas_call(kernel, out_shape=jax.ShapeDtypeStruct((2, TOK, H * DK), B...  68.6 us
    unnamed x1, local copies, waits for them, and re-layouts  2.29 us

profile of v4, /device:TPU:6, one launch (start us, length us, event | category | flops | bytes accessed | tf_op | source)
XLA Modules:
  0.0 70.9 jit_solution(17121580266340427802)
XLA Ops:
  0.0 68.6 %delta_attention.1 = bf16[2,64,4096]{2,1,0:T(8,128)(2,1)} custom-call(bf16[2,64,4096]{2,1,0:T(8,128)(2,1)} %q_in.1, bf16[2,64,4096]{2,1,0:T(8,128)(2,1)} %k_in.1, bf16[2,64,4096]{2,1,0:T(8,128)(2,1)} %v_in.1, bf16[2,32,64]{2,1,0:T(8,128)(2,1)} %bitcast.2, s32[2,64]{1,0:T(2,128)} %mark_in.1, s32[2,64]{1,0:T(2,128)} %kind_in.1, bf16[2,64,128]{2,1,0:T(8,128)(2,1)} %lat_in.1, ...), custom_call_target="tpu_custom_call" | custom-call | tf_op jit(solution)/shard_map/delta_attention/pallas_call | solution.py:531
  68.6 2.3 %copy.14 = bf16[2,64,4096]{2,1,0:T(8,128)(2,1)} copy(bf16[2,64,4096]{2,1,0:T(8,128)(2,1)} %delta_attention.1) | data formatting | bytes 2097152

commit v5 on v4

--- a/solution.py
+++ b/solution.py
@@ -1,5 +1,3 @@
-import functools
-
 import jax
 import jax.numpy as jnp
 from jax import lax
@@ -67,9 +65,10 @@
 
 
 def kernel(
-    q_in, k_in, v_in, beta_in, mark_in, kind_in, lat_in, up_in, bias_in, rate_in, gate_in, gain_in,
+    q_in, k_in, v_in, beta_hbm, mark_hbm, kind_hbm, lat_in, up_in, bias_in, rate_in, gate_in,
+    gain_hbm,
     out_ref,
-    kb, vb, qb, lb, auxb, aux_src, upb, biasb, gateb, scale,
+    beta_in, mark_in, kind_in, gain_in, kb, vb, qb, lb, auxb, aux_src, upb, biasb, gateb, scale,
     total, grow, shrink, keyg, tail, xb, wb, ub, mcb, ocb, right, cols, rows,
     maps, first, gathered, states, leftb, core_buf, back,
     send, recv, pre_send, pre_recv, back_send, back_recv, here,
@@ -84,6 +83,15 @@
     def owner_id(owner):
         return {"head": owner // 2, "seq": seq - core + lax.rem(owner, 2)}
 
+    small = (
+        pltpu.make_async_copy(beta_hbm, beta_in, here.at[3]),
+        pltpu.make_async_copy(mark_hbm, mark_in, here.at[4]),
+        pltpu.make_async_copy(kind_hbm, kind_in, here.at[5]),
+        pltpu.make_async_copy(gain_hbm, gain_in, here.at[6]),
+    )
+    for copy in small:
+        copy.start()
+
     barrier = pltpu.get_barrier_semaphore()
 
     def greet(step, carry):
@@ -117,11 +125,13 @@
     ti = lax.broadcasted_iota(jnp.int32, (TOK, C), 0)
     tj = lax.broadcasted_iota(jnp.int32, (TOK, C), 1)
     packed = jnp.zeros((8 * OWNERS, C), F32)
+    for copy in small:
+        copy.wait()
     for b in range(2):
-        small = dot(select, beta_in[b])
-        small = jnp.where(part == 1, mark_in[b:b + 1, :].astype(F32), small)
-        small = jnp.where(part == 2, kind_in[b:b + 1, :].astype(F32), small)
-        packed = packed + dot(small.astype(BF16), (tj == ti + b * TOK).astype(BF16))
+        tiny = dot(select, beta_in[b])
+        tiny = jnp.where(part == 1, mark_in[b:b + 1, :].astype(F32), tiny)
+        tiny = jnp.where(part == 2, kind_in[b:b + 1, :].astype(F32), tiny)
+        packed = packed + dot(tiny.astype(BF16), (tj == ti + b * TOK).astype(BF16))
     aux_src[...] = packed.reshape(OWNERS, 8, C).astype(BF16)
 
     pl.semaphore_wait(barrier, OWNERS + 2)
@@ -396,24 +406,24 @@
         live = query * (count_col < 0.5).astype(F32)
         return halves(jnp.concatenate([live, mix], axis=1))
 
-    def query_stage(step, carry, chain):
+    def query_stage(step, carry):
         for inner in range(4):
             j = step * 4 + inner
-            leftb[aligned(j * C, C), :] = jnp.concatenate(query_parts(chain, j), axis=1)
+            leftb[aligned(j * C, C), :] = jnp.concatenate(query_parts(0, j), axis=1)
         return carry
 
     arrived(4, qb.at[0])
-    lax.fori_loop(0, BLOCKS // 4, functools.partial(query_stage, chain=0), 0)
-
-    @pl.when(x == 0)
-    def _():
-        first[...] = jnp.zeros_like(first)
-
-    for src_x in range(3):
-
-        @pl.when(x > src_x)
+    lax.fori_loop(0, BLOCKS // 4, query_stage, 0)
+
+    def incoming_state(chain):
+        @pl.when(x == 0)
         def _():
-            for chain in range(2):
+            first[chain] = jnp.zeros((DK, DK), F32)
+
+        for src_x in range(3):
+
+            @pl.when(x > src_x)
+            def _():
                 map_copy(chain, src_x, src_x + 1).wait_recv()
                 if src_x == 0:
                     first[chain] = gathered[0, chain, :, DK:]
@@ -426,15 +436,14 @@
         mc = mcb[chain, at, :]
         return ocb[chain, at, :] + dot(jnp.concatenate([mc, mc[:, :C]], axis=1), incoming)
 
-    now = [first[0], first[1]]
-    for four in range(BLOCKS // 4):
-        for chain in range(2):
-            incoming = right_of(halves(now[chain]))
+    def state_stage(chain):
+        now = first[chain]
+        for four in range(BLOCKS // 4):
+            incoming = right_of(halves(now))
             states[chain, four] = incoming
             if four < BLOCKS // 4 - 1:
-                now[chain] = moved(chain, pl.ds(four * 4 * C, C), incoming)
-
-    def state_stage(chain):
+                now = moved(chain, pl.ds(four * 4 * C, C), incoming)
+
         def body(step, carry):
             todo = []
             for inner in range(8):
@@ -460,11 +469,13 @@
             for inner in range(4):
                 j = 4 * p + inner
                 at = aligned(j * C, C)
-                ls = leftb[at, :]
+                if chain == 0:
+                    ls = leftb[at, :]
+                    left = jnp.concatenate([ls, ls[:, :2 * C]], axis=1)
+                else:
+                    left = left_of(query_parts(chain, j))
                 hold = right[chain, j]
-                out = dot(
-                    jnp.concatenate([ls, ls[:, :2 * C]], axis=1), stack(hold[:2 * C], hold)
-                )
+                out = dot(left, stack(hold[:2 * C], hold))
                 core_buf[chain, at, :] = out.astype(BF16)
             for inner in range(8):
                 b = 8 * p + lax.rem(blk + inner, 8)
@@ -487,11 +498,12 @@
 
         lax.fori_loop(1, BLOCKS // 4, others, 0)
 
+    incoming_state(0)
     state_stage(0)
     output_stage(0)
+    incoming_state(1)
     state_stage(1)
     arrived(5, qb.at[1])
-    lax.fori_loop(0, BLOCKS // 4, functools.partial(query_stage, chain=1), 0)
     output_stage(1)
 
     for chain in range(2):
@@ -531,9 +543,13 @@
     return pl.pallas_call(
         kernel,
         out_shape=jax.ShapeDtypeStruct((2, TOK, H * DK), BF16),
-        in_specs=[ANY, ANY, ANY, VM, VM, VM, ANY, ANY, ANY, SM, ANY, VM],
+        in_specs=[ANY, ANY, ANY, ANY, ANY, ANY, ANY, ANY, ANY, SM, ANY, ANY],
         out_specs=VM,
         scratch_shapes=[
+            pltpu.VMEM((2, H, TOK), BF16),
+            pltpu.VMEM((2, TOK), jnp.int32),
+            pltpu.VMEM((2, TOK), jnp.int32),
+            pltpu.VMEM((1, H * DK), F32),
             span(DK, BF16), span(DK, BF16), span(DK, BF16), span(DK, BF16),
             pltpu.VMEM((OWNERS, 8, C), BF16),
             pltpu.VMEM((OWNERS, 8, C), BF16),
@@ -567,7 +583,7 @@
             pltpu.SemaphoreType.DMA((2, 3)),
             pltpu.SemaphoreType.DMA((2,)),
             pltpu.SemaphoreType.DMA((2,)),
-            pltpu.SemaphoreType.DMA((3,)),
+            pltpu.SemaphoreType.DMA((7,)),
         ],
         compiler_params=pltpu.CompilerParams(
             collective_id=0, has_side_effects=True, vmem_limit_bytes=60 * 1024 * 1024

time: 72 us -> 69.2 us (0.961)
  Pallas kernels: 68.6 us -> 66.3 us
    pallas_call x1, Pallas kernels: 68.6 us -> 66.3 us  [per_device(): pl.pallas_call(kernel, out_shape=jax.ShapeDtypeStruct((2, TOK, H * DK), B...]
where the time goes in v5:
time: 69.2 us; the launch traced here: 68.6 us
  Pallas kernels  66.3 us (96%)
  local copies, waits for them, and re-layouts  2.29 us (3%)
    pallas_call x1, Pallas kernels, per_device(): pl.pallas_call(kernel, out_shape=jax.ShapeDtypeStruct((2, TOK, H * DK), B...  66.3 us
    unnamed x1, local copies, waits for them, and re-layouts  2.29 us

profile of v5, /device:TPU:6, one launch (start us, length us, event | category | flops | bytes accessed | tf_op | source)
XLA Modules:
  0.0 68.6 jit_solution(6331675059822441849)
XLA Ops:
  0.0 66.3 %delta_attention.1 = bf16[2,64,4096]{2,1,0:T(8,128)(2,1)} custom-call(bf16[2,64,4096]{2,1,0:T(8,128)(2,1)} %q_in.1, bf16[2,64,4096]{2,1,0:T(8,128)(2,1)} %k_in.1, bf16[2,64,4096]{2,1,0:T(8,128)(2,1)} %v_in.1, bf16[2,32,64]{2,1,0:T(8,128)(2,1)} %bitcast.2, s32[2,64]{1,0:T(2,128)} %mark_hbm.1, s32[2,64]{1,0:T(2,128)} %kind_hbm.1, bf16[2,64,128]{2,1,0:T(8,128)(2,1)} %lat_in.1, ...), custom_call_target="tpu_custom_call" | custom-call | tf_op jit(solution)/shard_map/delta_attention/pallas_call | solution.py:543
  66.3 2.3 %copy.14 = bf16[2,64,4096]{2,1,0:T(8,128)(2,1)} copy(bf16[2,64,4096]{2,1,0:T(8,128)(2,1)} %delta_attention.1) | data formatting | bytes 2097152

commit v6 on v5

--- a/solution.py
+++ b/solution.py
@@ -20,7 +20,7 @@
 ANY = pl.BlockSpec(memory_space=pl.ANY)
 VM = pl.BlockSpec(memory_space=pltpu.VMEM)
 SM = pl.BlockSpec(memory_space=pltpu.SMEM)
-LAT, AUX, PASS = 6, 7, 8
+LAT, AUX, PASS = 6, 8, 9
 KEY_STEP = 8
 
 
@@ -51,8 +51,8 @@
 
 def softplus(x):
     u = jnp.exp(-jnp.abs(x))
-    series = u * (1.0 - u * (0.5 - u * (1.0 / 3.0 - u * 0.25)))
-    return jnp.maximum(x, 0.0) + jnp.where(u < 0.015625, series, jnp.log(1.0 + u))
+    series = u * (1.0 - u * (0.5 - u * (1.0 / 3.0)))
+    return jnp.maximum(x, 0.0) + jnp.where(u < 0.0078125, series, jnp.log(1.0 + u))
 
 
 def unit(x):
@@ -70,7 +70,7 @@
     out_ref,
     beta_in, mark_in, kind_in, gain_in, kb, vb, qb, lb, auxb, aux_src, upb, biasb, gateb, scale,
     total, grow, shrink, keyg, tail, xb, wb, ub, mcb, ocb, right, cols, rows,
-    maps, first, gathered, states, leftb, core_buf, back,
+    maps, first, maps_out, gathered, states, leftb, core_buf, back,
     send, recv, pre_send, pre_recv, back_send, back_recv, here,
 ):
     group = lax.axis_index("head")
@@ -136,15 +136,22 @@
 
     pl.semaphore_wait(barrier, OWNERS + 2)
 
-    def lat_send(step, carry):
-        pltpu.make_async_remote_copy(
-            lat_in, lb.at[:, my_rows, :], send.at[LAT], recv.at[LAT],
-            device_id={"head": lax.rem(group + 5 * step, GROUPS), "seq": seq}, device_id_type=MESH,
+    def lat_spread(chain):
+        def one(step, carry):
+            pltpu.make_async_remote_copy(
+                lat_in.at[chain], lb.at[chain, my_rows, :], send.at[LAT + chain],
+                recv.at[LAT + chain],
+                device_id={"head": lax.rem(group + 5 * step, GROUPS), "seq": seq},
+                device_id_type=MESH,
+            ).start()
+            return carry
+
+        lax.fori_loop(1, GROUPS, one, 0)
+        pltpu.make_async_copy(
+            lat_in.at[chain], lb.at[chain, my_rows, :], recv.at[LAT + chain]
         ).start()
-        return carry
-
-    lax.fori_loop(1, GROUPS, lat_send, 0)
-    pltpu.make_async_copy(lat_in, lb.at[:, my_rows, :], recv.at[LAT]).start()
+
+    lat_spread(0)
 
     def aux_send(step, carry):
         other = lax.rem(me + step, OWNERS)
@@ -156,6 +163,7 @@
 
     lax.fori_loop(1, OWNERS, aux_send, 0)
     pltpu.make_async_copy(aux_src.at[me], auxb.at[blk], recv.at[AUX]).start()
+    lat_spread(1)
 
     def spread(slot, src, dst, chain):
         def one(step, carry):
@@ -189,13 +197,17 @@
 
     lax.fori_loop(0, H // 4, gates, 0)
 
-    half = lb.at[:, aligned(core * (SPAN // 2), SPAN // 2), :]
-    arrived(LAT, half)
-    pass_on = pltpu.make_async_remote_copy(
-        half, half, send.at[PASS], recv.at[PASS],
-        device_id={"seq": seq + 1 - 2 * core}, device_id_type=MESH,
-    )
-    pass_on.start()
+    pass_on = []
+    for chain in range(2):
+        half = lb.at[chain, aligned(core * (SPAN // 2), SPAN // 2), :]
+        arrived(LAT + chain, half)
+        pass_on.append(
+            pltpu.make_async_remote_copy(
+                half, half, send.at[PASS + chain], recv.at[PASS + chain],
+                device_id={"seq": seq + 1 - 2 * core}, device_id_type=MESH,
+            )
+        )
+        pass_on[chain].start()
     spread(1, k_in, kb, 1)
     spread(2, v_in, vb, 0)
     spread(3, v_in, vb, 1)
@@ -215,10 +227,9 @@
 
     rate = -jnp.exp(jnp.full((1, DK), rate_in[me], F32))
 
-    def decays(step, start):
+    def small_rows(step, carry):
         for inner in range(4):
-            j = lax.rem(start + step * 4 + inner, BLOCKS)
-            at = aligned(j * C, C)
+            j = step * 4 + inner
             one = auxb[2 * j].astype(F32)
             two = auxb[2 * j + 1].astype(F32)
             mine = stack(
@@ -226,21 +237,25 @@
                 jnp.where(lane < TOK, pltpu.roll(one, TOK, 1), two),
             )
             counts = dot(mine.astype(BF16), upper)
-            tall = stack(jax.nn.sigmoid(mine), counts, mine, jnp.zeros((C - 48, C), F32)).T
-            cols[j] = tall
+            cols[j] = stack(jax.nn.sigmoid(mine), counts, mine, jnp.zeros((C - 48, C), F32)).T
             rows[j] = counts
-            for chain in range(2):
-                kind = tall[:, 34 + 8 * chain:35 + 8 * chain]
-                pre = dot(lb[chain, at, :], upb[...]).astype(BF16).astype(F32)
-                bias = jnp.where(kind > 0.5, biasb[1:2, :], biasb[0:1, :])
-                decay = rate * softplus(pre + bias)
-                dh, dl = halves(decay)
-                total[chain, at, :] = dot(tri2, stack(dh, dl))
-        return start
-
-    lax.fori_loop(0, BLOCKS // 8, decays, core * (BLOCKS // 2))
-    pass_on.wait()
-    lax.fori_loop(0, BLOCKS // 8, decays, (1 - core) * (BLOCKS // 2))
+        return carry
+
+    def decay_stage(chain, half_core):
+        for inner in range(BLOCKS // 2):
+            j = half_core * (BLOCKS // 2) + inner
+            at = aligned(j * C, C)
+            kind = cols[j, :, 34 + 8 * chain:35 + 8 * chain]
+            pre = dot(lb[chain, at, :], upb[...]).astype(BF16).astype(F32)
+            bias = jnp.where(kind > 0.5, biasb[1:2, :], biasb[0:1, :])
+            dh, dl = halves(rate * softplus(pre + bias))
+            total[chain, at, :] = dot(tri2, stack(dh, dl))
+
+    lax.fori_loop(0, BLOCKS // 4, small_rows, 0)
+    for chain in range(2):
+        decay_stage(chain, core)
+        pass_on[chain].wait()
+        decay_stage(chain, 1 - core)
 
     near = ((ri // 16) == (ci // 16)).astype(BF16)
     eye_wide = eye.astype(F32)
@@ -364,7 +379,7 @@
     def map_copy(chain, src_x, to):
         cut = pl.ds(DK, DK) if src_x == 0 else pl.ds(0, 2 * DK)
         return pltpu.make_async_remote_copy(
-            maps.at[chain, :, cut], gathered.at[src_x, chain, :, cut],
+            maps_out.at[chain, :, cut], gathered.at[src_x, chain, :, cut],
             pre_send.at[chain, to - 1], pre_recv.at[chain, src_x],
             device_id={"seq": 2 * to + core}, device_id_type=MESH,
         )
@@ -387,9 +402,11 @@
     key_stage(1)
     arrived(2, vb.at[0])
     value_stage(0)
+    maps_out[0] = maps[0].astype(BF16)
     map_sends(0, False)
     arrived(3, vb.at[1])
     value_stage(1)
+    maps_out[1] = maps[1].astype(BF16)
     map_sends(1, False)
 
     def query_parts(chain, j):
@@ -426,10 +443,11 @@
             def _():
                 map_copy(chain, src_x, src_x + 1).wait_recv()
                 if src_x == 0:
-                    first[chain] = gathered[0, chain, :, DK:]
+                    first[chain] = gathered[0, chain, :, DK:].astype(F32)
                 else:
-                    first[chain] = gathered[src_x, chain, :, DK:] + fine(
-                        halves(gathered[src_x, chain, :, 0:DK]), halves(first[chain])
+                    move = gathered[src_x, chain, :, 0:DK]
+                    first[chain] = gathered[src_x, chain, :, DK:].astype(F32) + dot(
+                        jnp.concatenate([move, move], axis=1), stack(*halves(first[chain]))
                     )
 
     def moved(chain, at, incoming):
@@ -529,8 +547,9 @@
     for chain in range(2):
         sent = back.at[0, :, pl.ds(0, many)]
         pltpu.make_async_copy(sent, sent, back_send.at[chain]).wait()
-    lat_sent = lb.at[:, pl.ds(0, (GROUPS - 1) * TOK), :]
-    pltpu.make_async_copy(lat_sent, lat_sent, send.at[LAT]).wait()
+    for chain in range(2):
+        lat_sent = lb.at[chain, pl.ds(0, (GROUPS - 1) * TOK), :]
+        pltpu.make_async_copy(lat_sent, lat_sent, send.at[LAT + chain]).wait()
     aux_sent = aux_src.at[pl.ds(0, OWNERS - 1)]
     pltpu.make_async_copy(aux_sent, aux_sent, send.at[AUX]).wait()
 
@@ -542,7 +561,7 @@
     span = lambda width, dtype: pltpu.VMEM((2, SPAN, width), dtype)
     return pl.pallas_call(
         kernel,
-        out_shape=jax.ShapeDtypeStruct((2, TOK, H * DK), BF16),
+        out_shape=pltpu.VMEM((2, TOK, H * DK), BF16),
         in_specs=[ANY, ANY, ANY, ANY, ANY, ANY, ANY, ANY, ANY, SM, ANY, ANY],
         out_specs=VM,
         scratch_shapes=[
@@ -572,13 +591,14 @@
             pltpu.VMEM((BLOCKS, 16, C), F32),
             pltpu.VMEM((2, DK, 2 * DK), F32),
             pltpu.VMEM((2, DK, DK), F32),
-            pltpu.VMEM((3, 2, DK, 2 * DK), F32),
+            pltpu.VMEM((2, DK, 2 * DK), BF16),
+            pltpu.VMEM((3, 2, DK, 2 * DK), BF16),
             pltpu.VMEM((2, BLOCKS // 4, 3 * C, DK), BF16),
             pltpu.VMEM((SPAN, 4 * C), BF16),
             span(DK, BF16),
             pltpu.VMEM((2, TOK, H * DK), BF16),
-            pltpu.SemaphoreType.DMA((9,)),
-            pltpu.SemaphoreType.DMA((9,)),
+            pltpu.SemaphoreType.DMA((11,)),
+            pltpu.SemaphoreType.DMA((11,)),
             pltpu.SemaphoreType.DMA((2, 3)),
             pltpu.SemaphoreType.DMA((2, 3)),
             pltpu.SemaphoreType.DMA((2,)),

time: 69.2 us -> 66.8 us (0.965)
  local copies, waits for them, and re-layouts: 2.29 us -> 0.97 us
  Pallas kernels: 66.3 us -> 65.5 us
    unnamed x1, local copies, waits for them, and re-layouts: 2.29 us -> 0.97 us
    pallas_call x1, Pallas kernels: 66.3 us -> 65.5 us  [per_device(): pl.pallas_call(kernel, out_shape=pltpu.VMEM((2, TOK, H * DK), BF16), in_s...]
where the time goes in v6:
time: 66.8 us; the launch traced here: 66.4 us
  Pallas kernels  65.5 us (98%)
  local copies, waits for them, and re-layouts  0.97 us (1%)
    pallas_call x1, Pallas kernels, per_device(): pl.pallas_call(kernel, out_shape=pltpu.VMEM((2, TOK, H * DK), BF16), in_s...  65.5 us

profile of v6, /device:TPU:6, one launch (start us, length us, event | category | flops | bytes accessed | tf_op | source)
XLA Modules:
  0.0 66.4 jit_solution(6471536706867303879)
XLA Ops:
  0.0 65.5 %delta_attention.1 = bf16[2,64,4096]{2,1,0:T(8,128)(2,1)S(1)} custom-call(bf16[2,64,4096]{2,1,0:T(8,128)(2,1)} %q_in.1, bf16[2,64,4096]{2,1,0:T(8,128)(2,1)} %k_in.1, bf16[2,64,4096]{2,1,0:T(8,128)(2,1)} %v_in.1, bf16[2,32,64]{2,1,0:T(8,128)(2,1)} %bitcast.2, s32[2,64]{1,0:T(2,128)} %mark_hbm.1, s32[2,64]{1,0:T(2,128)} %kind_hbm.1, ...), custom_call_target="tpu_custom_call" | custom-call | tf_op jit(solution)/shard_map/delta_attention/pallas_call | solution.py:562
  65.5 1.0 %copy.14 = bf16[2,64,4096]{2,1,0:T(8,128)(2,1)} copy(bf16[2,64,4096]{2,1,0:T(8,128)(2,1)S(1)} %delta_attention.1) | data formatting | bytes 2097152

commit v7 on v6

--- a/solution.py
+++ b/solution.py
@@ -70,7 +70,7 @@
     out_ref,
     beta_in, mark_in, kind_in, gain_in, kb, vb, qb, lb, auxb, aux_src, upb, biasb, gateb, scale,
     total, grow, shrink, keyg, tail, xb, wb, ub, mcb, ocb, right, cols, rows,
-    maps, first, maps_out, gathered, states, leftb, core_buf, back,
+    maps, first, maps_out, gathered, states, core_buf, back,
     send, recv, pre_send, pre_recv, back_send, back_recv, here,
 ):
     group = lax.axis_index("head")
@@ -96,7 +96,7 @@
 
     def greet(step, carry):
         pl.semaphore_signal(
-            barrier, inc=1, device_id=owner_id(lax.rem(me + step, OWNERS)), device_id_type=MESH
+            barrier, inc=1, device_id=owner_id(lax.rem(me + 21 * step, OWNERS)), device_id_type=MESH
         )
         return carry
 
@@ -115,6 +115,25 @@
     )
     for copy in local:
         copy.start()
+
+    pl.semaphore_wait(barrier, OWNERS + 2)
+
+    def lat_spread(chain):
+        def one(step, carry):
+            pltpu.make_async_remote_copy(
+                lat_in.at[chain], lb.at[chain, my_rows, :], send.at[LAT + chain],
+                recv.at[LAT + chain],
+                device_id={"head": lax.rem(group + 5 * step, GROUPS), "seq": seq},
+                device_id_type=MESH,
+            ).start()
+            return carry
+
+        lax.fori_loop(1, GROUPS, one, 0)
+        pltpu.make_async_copy(
+            lat_in.at[chain], lb.at[chain, my_rows, :], recv.at[LAT + chain]
+        ).start()
+
+    lat_spread(0)
 
     ri = lax.broadcasted_iota(jnp.int32, (C, C), 0)
     ci = lax.broadcasted_iota(jnp.int32, (C, C), 1)
@@ -133,25 +152,6 @@
         tiny = jnp.where(part == 2, kind_in[b:b + 1, :].astype(F32), tiny)
         packed = packed + dot(tiny.astype(BF16), (tj == ti + b * TOK).astype(BF16))
     aux_src[...] = packed.reshape(OWNERS, 8, C).astype(BF16)
-
-    pl.semaphore_wait(barrier, OWNERS + 2)
-
-    def lat_spread(chain):
-        def one(step, carry):
-            pltpu.make_async_remote_copy(
-                lat_in.at[chain], lb.at[chain, my_rows, :], send.at[LAT + chain],
-                recv.at[LAT + chain],
-                device_id={"head": lax.rem(group + 5 * step, GROUPS), "seq": seq},
-                device_id_type=MESH,
-            ).start()
-            return carry
-
-        lax.fori_loop(1, GROUPS, one, 0)
-        pltpu.make_async_copy(
-            lat_in.at[chain], lb.at[chain, my_rows, :], recv.at[LAT + chain]
-        ).start()
-
-    lat_spread(0)
 
     def aux_send(step, carry):
         other = lax.rem(me + step, OWNERS)
@@ -423,15 +423,6 @@
         live = query * (count_col < 0.5).astype(F32)
         return halves(jnp.concatenate([live, mix], axis=1))
 
-    def query_stage(step, carry):
-        for inner in range(4):
-            j = step * 4 + inner
-            leftb[aligned(j * C, C), :] = jnp.concatenate(query_parts(0, j), axis=1)
-        return carry
-
-    arrived(4, qb.at[0])
-    lax.fori_loop(0, BLOCKS // 4, query_stage, 0)
-
     def incoming_state(chain):
         @pl.when(x == 0)
         def _():
@@ -487,23 +478,18 @@
             for inner in range(4):
                 j = 4 * p + inner
                 at = aligned(j * C, C)
-                if chain == 0:
-                    ls = leftb[at, :]
-                    left = jnp.concatenate([ls, ls[:, :2 * C]], axis=1)
-                else:
-                    left = left_of(query_parts(chain, j))
                 hold = right[chain, j]
-                out = dot(left, stack(hold[:2 * C], hold))
+                out = dot(left_of(query_parts(chain, j)), stack(hold[:2 * C], hold))
                 core_buf[chain, at, :] = out.astype(BF16)
             for inner in range(8):
                 b = 8 * p + lax.rem(blk + inner, 8)
                 src = core_buf.at[chain, aligned(b * TOK, TOK), :]
                 dst = back.at[chain, :, my_cols]
                 if own and inner == 0:
-                    pltpu.make_async_copy(src, dst, back_recv.at[chain]).start()
+                    pltpu.make_async_copy(src, dst, back_recv.at[chain, 0]).start()
                 else:
                     pltpu.make_async_remote_copy(
-                        src, dst, back_send.at[chain], back_recv.at[chain],
+                        src, dst, back_send.at[chain], back_recv.at[chain, step],
                         device_id={"head": lax.rem(b, GROUPS), "seq": seq - core + b // GROUPS},
                         device_id_type=MESH,
                     ).start()
@@ -518,6 +504,7 @@
 
     incoming_state(0)
     state_stage(0)
+    arrived(4, qb.at[0])
     output_stage(0)
     incoming_state(1)
     state_stage(1)
@@ -525,17 +512,20 @@
     output_stage(1)
 
     for chain in range(2):
-        pltpu.make_async_copy(back.at[chain], back.at[chain], back_recv.at[chain]).wait()
 
         def finish(step, carry, chain=chain):
+            some = back.at[chain, :, pl.ds(0, 8 * DK)]
+            pltpu.make_async_copy(some, some, back_recv.at[chain, step]).wait()
+            q = lax.rem(blk // 8 + 4 - step, 4)
+            base = lax.rem(q, 2) * 16 + q // 2
             for inner in range(8):
-                at = aligned((step * 8 + inner) * DK, DK)
+                at = aligned((base + 2 * inner) * DK, DK)
                 wide = back[chain, :, at].astype(F32)
                 norm = lax.rsqrt(jnp.mean(wide * wide, axis=-1, keepdims=True) + NORM_EPS)
                 out_ref[chain, :, at] = (wide * norm * scale[chain, :, at]).astype(BF16)
             return carry
 
-        lax.fori_loop(0, H // 8, finish, 0)
+        lax.fori_loop(0, 4, finish, 0)
 
     map_sends(0, True)
     map_sends(1, True)
@@ -594,7 +584,6 @@
             pltpu.VMEM((2, DK, 2 * DK), BF16),
             pltpu.VMEM((3, 2, DK, 2 * DK), BF16),
             pltpu.VMEM((2, BLOCKS // 4, 3 * C, DK), BF16),
-            pltpu.VMEM((SPAN, 4 * C), BF16),
             span(DK, BF16),
             pltpu.VMEM((2, TOK, H * DK), BF16),
             pltpu.SemaphoreType.DMA((11,)),
@@ -602,7 +591,7 @@
             pltpu.SemaphoreType.DMA((2, 3)),
             pltpu.SemaphoreType.DMA((2, 3)),
             pltpu.SemaphoreType.DMA((2,)),
-            pltpu.SemaphoreType.DMA((2,)),
+            pltpu.SemaphoreType.DMA((2, 4)),
             pltpu.SemaphoreType.DMA((7,)),
         ],
         compiler_params=pltpu.CompilerParams(

time: 66.8 us -> 66 us (0.988)
  no operation moved by 1% of the time
where the time goes in v7:
time: 66 us; the launch traced here: 65.9 us
  Pallas kernels  64.9 us (98%)
  local copies, waits for them, and re-layouts  0.97 us (1%)
    pallas_call x1, Pallas kernels, per_device(): pl.pallas_call(kernel, out_shape=pltpu.VMEM((2, TOK, H * DK), BF16), in_s...  64.9 us

profile of v7, /device:TPU:6, one launch (start us, length us, event | category | flops | bytes accessed | tf_op | source)
XLA Modules:
  0.0 65.9 jit_solution(573373972546766765)
XLA Ops:
  0.0 64.9 %delta_attention.1 = bf16[2,64,4096]{2,1,0:T(8,128)(2,1)S(1)} custom-call(bf16[2,64,4096]{2,1,0:T(8,128)(2,1)} %q_in.1, bf16[2,64,4096]{2,1,0:T(8,128)(2,1)} %k_in.1, bf16[2,64,4096]{2,1,0:T(8,128)(2,1)} %v_in.1, bf16[2,32,64]{2,1,0:T(8,128)(2,1)} %bitcast.2, s32[2,64]{1,0:T(2,128)} %mark_hbm.1, s32[2,64]{1,0:T(2,128)} %kind_hbm.1, ...), custom_call_target="tpu_custom_call" | custom-call | tf_op jit(solution)/shard_map/delta_attention/pallas_call | solution.py:552
  64.9 1.0 %copy.14 = bf16[2,64,4096]{2,1,0:T(8,128)(2,1)} copy(bf16[2,64,4096]{2,1,0:T(8,128)(2,1)S(1)} %delta_attention.1) | data formatting | bytes 2097152

commit v8 on v7

--- a/solution.py
+++ b/solution.py
@@ -208,7 +208,8 @@
             )
         )
         pass_on[chain].start()
-    spread(1, k_in, kb, 1)
+        if chain == 0:
+            spread(1, k_in, kb, 1)
     spread(2, v_in, vb, 0)
     spread(3, v_in, vb, 1)
     spread(4, q_in, qb, 0)

time: 66 us -> 65.6 us (level)
  no operation moved by 1% of the time
where the time goes in v8:
time: 65.6 us; the launch traced here: 65.5 us
  Pallas kernels  64.5 us (98%)
  local copies, waits for them, and re-layouts  0.97 us (1%)
    pallas_call x1, Pallas kernels, per_device(): pl.pallas_call(kernel, out_shape=pltpu.VMEM((2, TOK, H * DK), BF16), in_s...  64.5 us

profile of v8, /device:TPU:6, one launch (start us, length us, event | category | flops | bytes accessed | tf_op | source)
XLA Modules:
  0.0 65.5 jit_solution(14275890522295617277)
XLA Ops:
  0.0 64.5 %delta_attention.1 = bf16[2,64,4096]{2,1,0:T(8,128)(2,1)S(1)} custom-call(bf16[2,64,4096]{2,1,0:T(8,128)(2,1)} %q_in.1, bf16[2,64,4096]{2,1,0:T(8,128)(2,1)} %k_in.1, bf16[2,64,4096]{2,1,0:T(8,128)(2,1)} %v_in.1, bf16[2,32,64]{2,1,0:T(8,128)(2,1)} %bitcast.2, s32[2,64]{1,0:T(2,128)} %mark_hbm.1, s32[2,64]{1,0:T(2,128)} %kind_hbm.1, ...), custom_call_target="tpu_custom_call" | custom-call | tf_op jit(solution)/shard_map/delta_attention/pallas_call | solution.py:553
  64.5 1.0 %copy.14 = bf16[2,64,4096]{2,1,0:T(8,128)(2,1)} copy(bf16[2,64,4096]{2,1,0:T(8,128)(2,1)S(1)} %delta_attention.1) | data formatting | bytes 2097152
